TPU v7x, 32 devices: a whole 2x2x4 slice. The times are simulated.
32 devices in a mesh: dp: 8 (over z, core), seq: 4 (over y, x).
Axes of the slice: x: 2, y: 2, z: 4, core: 2. Of those that a mesh axis runs over, the one named last changes fastest.
Arguments:
- tokens: int32 [8, 65536], P('dp', 'seq'), may hold values from 0 to 4
- stem_weight: bfloat16 [60, 768], replicated, may hold values from -1.5 to 1.5
- stem_bias: float32 [768], replicated, may hold values from -3 to 3
- conv_gain: float32 [768], replicated, may hold values from 0.1 to 1.9
- conv_weight: bfloat16 [5, 768, 1536], P(None, 'dp'), may hold values from -0.09375 to 0.09375
- conv_bias: float32 [1536], replicated, may hold values from -3 to 3
- attn_gain: float32 [1536], replicated, may hold values from 0.1 to 1.9
- w_query: bfloat16 [1536, 1024], P('dp'), may hold values from -7 to 7
- w_key: bfloat16 [1536, 128], P('dp'), may hold values from -0.15625 to 0.15625
- w_value: bfloat16 [1536, 192], P('dp'), may hold values from -0.15625 to 0.15625
- w_out: bfloat16 [1536, 1536], P('dp'), may hold values from -0.4375 to 0.4375
Outputs:
- features: bfloat16 [8, 512, 1536], P('dp', 'seq')
Inputs may be any that keep to these rules, and one draw needn't show every extreme that they name: `tokens`: 0 is an unknown base; 1 to 4 are A, C, G, T.
All inputs are finite; a program needn't handle non-finite values.
Results may differ from a plain program's by a relative error of at most 0.009.
The roundings to bfloat16 on the way count: a program that leaves them out, or rounds other values in their place, can miss the bound.
Values may be sent and summed in bfloat16 or wider, within the bound.
A program may use at most 192 MiB of HBM per device.

v0:
```python
import functools

import jax
import jax.numpy as jnp
from jax import lax
from jax.experimental import pallas as pl
from jax.experimental.pallas import tpu as pltpu
from jax.sharding import PartitionSpec as P

HEADS = 8
HEAD_K = 128
HEAD_V = 192
KW_STEM = 15
KW = 5
POOL_A = 8
POOL_B = 16
GROUP = POOL_A * POOL_B
SPAN = 24

epsilon = 1e-06


def rms_scale(values, gain):
    return values * lax.rsqrt(jnp.mean(values * values, axis=-1, keepdims=True) + epsilon) * gain


def rotate(values, angles):
    half_dim = values.shape[-1] // 2
    first = values[..., :half_dim]
    second = values[..., half_dim:]
    cosine = jnp.cos(angles)
    sine = jnp.sin(angles)
    return jnp.concatenate(
        [first * cosine - second * sine, second * cosine + first * sine], axis=-1
    )


def stem_kernel(
    tok_ref, low_ref, high_ref, weight_ref, bias_ref, gain_ref, ext_ref, text_ref, hot_ref, shifted_ref, rows_ref
):
    stem_compute(
        tok_ref,
        low_ref[...],
        high_ref[...],
        weight_ref,
        bias_ref,
        gain_ref,
        ext_ref,
        text_ref,
        hot_ref,
        shifted_ref,
        rows_ref,
    )


def stem_compute(
    tok_ref, low, high, weight_ref, bias_ref, gain_ref, ext_ref, text_ref, hot_ref, shifted_ref, rows_ref, between=None
):
    count = tok_ref.shape[0]
    channels = weight_ref.shape[1]
    place = lax.axis_index("seq")
    last_place = lax.axis_size("seq") - 1
    main = tok_ref[...].astype(jnp.float32)
    row = lax.broadcasted_iota(jnp.int32, main.shape, 0)
    previous = jnp.where(row == 0, low.astype(jnp.float32), pltpu.roll(main, 1, 0))
    following = jnp.where(
        row == count - 1, high.astype(jnp.float32), pltpu.roll(main, count - 1, 0)
    )
    text_ref[0:SPAN, :] = previous.T[GROUP - SPAN :, :]
    text_ref[SPAN : SPAN + GROUP, :] = main.T
    text_ref[SPAN + GROUP :, :] = following.T[:SPAN, :]

    source = lax.broadcasted_iota(jnp.int32, (GROUP, weight_ref.shape[0]), 1)
    target = lax.broadcasted_iota(jnp.int32, (GROUP, weight_ref.shape[0]), 0)
    tap = source // 4
    base = source - 4 * tap
    for offset in range(POOL_A):
        pick = (target == base * SPAN + offset + tap + 1).astype(jnp.float32).astype(jnp.bfloat16)
        shifted_ref[offset] = jnp.dot(
            pick, weight_ref[...], preferred_element_type=jnp.float32
        ).astype(jnp.bfloat16)

    def hot_of(span):
        planes = [(span == float(code)).astype(jnp.float32) for code in range(1, 5)]
        planes.append(jnp.zeros((GROUP - 4 * SPAN, span.shape[1]), jnp.float32))
        return jnp.concatenate(planes, axis=0).T.astype(jnp.bfloat16)

    for j in range(POOL_B):
        hot_ref[j] = hot_of(text_ref[8 * j + SPAN - 8 : 8 * j + 2 * SPAN - 8, :])
    lane = lax.broadcasted_iota(jnp.int32, (SPAN, count), 1)
    edge = jnp.where(
        lane == 0,
        text_ref[0:SPAN, :],
        jnp.where(
            lane == 1,
            pltpu.roll(text_ref[8 : 8 + SPAN, :], 1, 1),
            jnp.where(
                lane == 2,
                pltpu.roll(text_ref[GROUP + SPAN - 8 : GROUP + 2 * SPAN - 8, :], 3, 1),
                pltpu.roll(text_ref[GROUP + SPAN : GROUP + 2 * SPAN, :], 4, 1),
            ),
        ),
    )
    hot_ref[POOL_B] = hot_of(edge)

    width = 256

    def block(j, carry):
        hot = hot_ref[j]
        for chunk in range(channels // width):
            columns = slice(chunk * width, (chunk + 1) * width)
            best = None
            for offset in range(POOL_A):
                stem = jnp.dot(
                    hot, shifted_ref[offset, :, columns], preferred_element_type=jnp.float32
                )
                best = stem if best is None else jnp.maximum(best, stem)
            pooled = jax.nn.gelu(best + bias_ref[:, columns]).astype(jnp.bfloat16)
            rows_ref[:, columns] = pooled.astype(jnp.float32)
        pooled = rows_ref[...]
        start = pl.multiple_of((j + 2) * count, count)
        ext_ref[pl.ds(start, count), :] = rms_scale(pooled, gain_ref[...]).astype(jnp.bfloat16)
        return carry

    if between is None:
        lax.fori_loop(0, POOL_B + 1, block, 0)
    else:
        lax.fori_loop(0, POOL_B // 2, block, 0)
        between()
        lax.fori_loop(POOL_B // 2, POOL_B + 1, block, 0)
    edges = ext_ref[(POOL_B + 2) * count : (POOL_B + 3) * count, :].astype(jnp.float32)
    left_keep = (place > 0).astype(jnp.float32)
    right_keep = (place < last_place).astype(jnp.float32)
    spot = lax.broadcasted_iota(jnp.int32, (count, channels), 0)
    for index in range(2):
        inner = ext_ref[(POOL_B + index) * count : (POOL_B + index + 1) * count, :]
        moved = pltpu.roll(inner.astype(jnp.float32), 1, 0)
        ext_ref[index * count : (index + 1) * count, :] = jnp.where(
            spot == 0, edges[index : index + 1, :] * left_keep, moved
        ).astype(jnp.bfloat16)
        inner = ext_ref[(2 + index) * count : (3 + index) * count, :]
        moved = pltpu.roll(inner.astype(jnp.float32), count - 1, 0)
        at = POOL_B + 2 + index
        ext_ref[at * count : (at + 1) * count, :] = jnp.where(
            spot == count - 1, edges[2 + index : 3 + index, :] * right_keep, moved
        ).astype(jnp.bfloat16)


def stem_stage(tokens, low, high, stem_weight, stem_bias, conv_gain):
    count = tokens.shape[0]
    channels = stem_weight.shape[1]
    return pl.pallas_call(
        stem_kernel,
        out_shape=jax.ShapeDtypeStruct(((POOL_B + 4) * count, channels), jnp.bfloat16),
        in_specs=[pl.BlockSpec(memory_space=pltpu.VMEM)] * 6,
        out_specs=pl.BlockSpec(memory_space=pltpu.VMEM),
        scratch_shapes=[
            pltpu.VMEM((GROUP + 2 * SPAN, count), jnp.float32),
            pltpu.VMEM((POOL_B + 1, count, GROUP), jnp.bfloat16),
            pltpu.VMEM((POOL_A, GROUP, channels), jnp.bfloat16),
            pltpu.VMEM((count, channels), jnp.float32),
        ],
        cost_estimate=pl.CostEstimate(
            flops=20_000_000_000, bytes_accessed=4_000_000, transcendentals=1_600_000
        ),
        name="stem_stage",
    )(tokens, low, high, stem_weight, stem_bias[None], conv_gain[None])


def conv_kernel(count, ext_ref, weight_ref, bias_ref, coarse_ref):
    group = 4
    width = weight_ref.shape[-1]
    channels = ext_ref.shape[1]

    def block(m, carry):
        most, least = carry
        total = None
        for tap in range(KW):
            start = pl.multiple_of((m * group + tap) * count, count)
            part = jnp.dot(
                ext_ref[pl.ds(start, group * count), :],
                weight_ref[:, :, 0, tap].reshape(channels, width),
                preferred_element_type=jnp.float32,
            )
            total = part if total is None else total + part
        for index in range(group):
            piece = total[index * count : (index + 1) * count]
            most = jnp.maximum(most, piece)
            least = jnp.minimum(least, piece)
        return most, least

    big = jnp.full((count, width), jnp.finfo(jnp.float32).max, jnp.float32)
    most, least = lax.fori_loop(0, POOL_B // group, block, (-big, big))
    bias = bias_ref[...]
    coarse_ref[...] = jnp.maximum(jax.nn.gelu(most + bias), jax.nn.gelu(least + bias)).astype(
        jnp.bfloat16
    )


def conv_stage(ext, weight, conv_bias):
    count = ext.shape[0] // (POOL_B + 4)
    ways, row_parts, column_parts, taps, depth, columns = weight.shape
    width = 256
    steps = columns // width
    return pl.pallas_call(
        functools.partial(conv_kernel, count),
        grid=(column_parts, steps),
        out_shape=jax.ShapeDtypeStruct((count, column_parts * columns), jnp.bfloat16),
        in_specs=[
            pl.BlockSpec(ext.shape, lambda b, n: (0, 0), pipeline_mode=pl.Buffered(1)),
            pl.BlockSpec(
                (ways, row_parts, 1, taps, depth, width), lambda b, n: (0, 0, b, 0, 0, n)
            ),
            pl.BlockSpec((1, width), lambda b, n: (0, b * steps + n)),
        ],
        out_specs=pl.BlockSpec((count, width), lambda b, n: (0, b * steps + n)),
        cost_estimate=pl.CostEstimate(
            flops=24_000_000_000, bytes_accessed=16_000_000, transcendentals=400_000
        ),
        name="conv_stage",
    )(ext, weight, conv_bias[None])


MESH = pl.DeviceIdType.MESH


def encoder_kernel(
    tok_ref,
    stem_weight_ref,
    vector_ref,
    cosine_ref,
    sine_ref,
    conv_ref,
    attn_ref,
    out_ref,
    coarse_ref,
    key_ref,
    value_ref,
    pair_send,
    pair_recv,
    text_ref,
    hot_ref,
    shifted_ref,
    rows_ref,
    ext_ref,
    low_ref,
    high_ref,
    conv_full,
    attn_full,
    halo_send,
    halo_recv,
    send_sem,
    recv_sem,
    half_sem,
    local_sem,
):
    stem_wide = stem_weight_ref.shape[1]
    wide = out_ref.shape[1]
    stem_bias_ref = vector_ref.at[:, 0:stem_wide]
    gain_ref = vector_ref.at[:, stem_wide : 2 * stem_wide]
    conv_bias_ref = vector_ref.at[:, 2 * stem_wide : 2 * stem_wide + wide]
    attn_gain_ref = vector_ref.at[:, 2 * stem_wide + wide :]
    ways = lax.axis_size("dp")
    members = lax.axis_size("seq")
    chips = ways // 2
    me = lax.axis_index("dp")
    place = lax.axis_index("seq")
    chip = me // 2
    core = me % 2
    partner = chip * 2 + 1 - core
    count = tok_ref.shape[0]
    _, row_parts, column_parts, _, _, columns = conv_full.shape
    depth = conv_full.shape[4]

    def peer_of(step):
        return (chip + step) % chips * 2 + core

    barrier = pltpu.get_barrier_semaphore()
    pl.semaphore_signal(barrier, inc=1, device_id=(partner, place), device_id_type=MESH)
    for step in range(1, chips):
        pl.semaphore_signal(
            barrier, inc=1, device_id=(peer_of(step), place), device_id_type=MESH
        )
    for turn in range(1, members):
        pl.semaphore_signal(
            barrier, inc=1, device_id=(me, (place + turn) % members), device_id_type=MESH
        )
    pl.semaphore_wait(barrier, 1 + (chips - 1) + (members - 1))

    right = (place + 1) % members
    left = (place + members - 1) % members
    halo = [
        pltpu.make_async_remote_copy(
            tok_ref.at[count - 8 : count], low_ref, halo_send.at[0], halo_recv.at[0], (me, right), MESH
        ),
        pltpu.make_async_remote_copy(
            tok_ref.at[0:8], high_ref, halo_send.at[1], halo_recv.at[1], (me, left), MESH
        ),
    ]
    for copy in halo:
        copy.start()

    def conv_source(spot):
        rows = pl.multiple_of(spot // column_parts * depth, depth)
        at = pl.multiple_of(spot % column_parts * columns, columns)
        return conv_ref.at[:, pl.ds(rows, depth), pl.ds(at, columns)]

    def conv_slot(way, spot):
        return conv_full.at[way, spot // column_parts, spot % column_parts]

    def attn_source(spot):
        return attn_ref.at[spot]

    def attn_slot(way, spot):
        return attn_full.at[way, spot]

    def conv_half(way, spot, half, turn):
        cut = columns // 256 * 128
        where = pl.ds(0, cut) if half == 0 else pl.ds(cut, columns - cut)
        return conv_full.at[way, spot // column_parts, spot % column_parts, :, :, where]

    def attn_half(way, spot, half, turn):
        rows = attn_ref.shape[1]
        tiles = rows // 16
        cut = (tiles // 2 if turn % 2 else tiles - tiles // 2) * 16
        where = pl.ds(0, cut) if half == 0 else pl.ds(cut, rows - cut)
        return attn_full.at[way, spot, where]

    kinds = ((conv_source, conv_slot, conv_half), (attn_source, attn_slot, attn_half))
    along_x = place + 1 - 2 * (place % 2)
    along_y = place + 2 - 4 * (place // 2)
    across = 3 - place
    sent = ([], [])
    local = ([], [])

    def send(kind, source, way, spot, target):
        copy = pltpu.make_async_remote_copy(
            source,
            kinds[kind][1](way, spot),
            send_sem.at[kind, len(sent[kind])],
            recv_sem.at[kind, way, spot],
            target,
            MESH,
        )
        copy.start()
        sent[kind].append(copy)

    def arrived(kind, way, spot):
        slot = kinds[kind][1](way, spot)
        pltpu.make_async_remote_copy(
            slot, slot, send_sem.at[kind, 0], recv_sem.at[kind, way, spot], (partner, place), MESH
        ).wait_recv()

    def first(kind):
        source, slot, _ = kinds[kind]
        for step in range(1, chips):
            send(kind, source(place), me, place, (peer_of(step), place))
        for spot in range(members):
            send(kind, source(spot), me, spot, (partner, place))
            copy = pltpu.make_async_copy(source(spot), slot(me, spot), local_sem.at[kind, spot])
            copy.start()
            local[kind].append(copy)

    order = sorted(range(1, chips), key=lambda step: min(step, chips - step))

    def second(kind, some):
        slot = kinds[kind][1]
        for step in some:
            way = peer_of(step)
            arrived(kind, way, place)
            send(kind, slot(way, place), way, place, (me, along_x))
            send(kind, slot(way, place), way, place, (me, along_y))
            send(kind, slot(way, place), way, place, (partner, place))

    def send_half(kind, way, spot, half, turn, target):
        ref = kinds[kind][2](way, spot, half, turn)
        copy = pltpu.make_async_remote_copy(
            ref,
            ref,
            send_sem.at[kind, len(sent[kind])],
            half_sem.at[kind, way, half],
            (me, target),
            MESH,
        )
        copy.start()
        sent[kind].append(copy)

    def third(kind):
        slot = kinds[kind][1]
        for turn, step in enumerate(order):
            way = peer_of(step)
            arrived(kind, way, along_x)
            send_half(kind, way, along_x, 0, turn, along_y)
            send(kind, slot(way, along_x), way, along_x, (partner, place))
            arrived(kind, way, along_y)
            send_half(kind, way, along_y, 1, turn, along_x)
            send(kind, slot(way, along_y), way, along_y, (partner, place))

    def fourth(kind):
        slot, half_of = kinds[kind][1:]
        for turn, step in enumerate(order):
            way = peer_of(step)
            for half in range(2):
                ref = half_of(way, across, half, turn)
                pltpu.make_async_remote_copy(
                    ref, ref, send_sem.at[kind, 0], half_sem.at[kind, way, half], (partner, place), MESH
                ).wait_recv()
            send(kind, slot(way, across), way, across, (partner, place))

    def finish(kind):
        for step in range(chips):
            way = (chip + step) % chips * 2 + 1 - core
            for spot in range(members):
                arrived(kind, way, spot)
        for copy in local[kind]:
            copy.wait()
        for copy in sent[kind]:
            copy.wait_send()

    first(0)
    for copy in halo:
        copy.wait()
    low = jnp.where(place > 0, low_ref[7:8], 0)
    high = jnp.where(place < members - 1, high_ref[0:1], 0)
    stem_compute(
        tok_ref,
        low,
        high,
        stem_weight_ref,
        stem_bias_ref,
        gain_ref,
        ext_ref,
        text_ref,
        hot_ref,
        shifted_ref,
        rows_ref,
        lambda: second(0, order[:1]),
    )
    second(0, order[1:])
    first(1)
    third(0)
    second(1, order[:1])
    fourth(0)
    second(1, order[1:])
    finish(0)

    width = 256
    steps = columns // width
    group = 8
    channels = ext_ref.shape[1]
    big = jnp.full((count, width), jnp.finfo(jnp.float32).max, jnp.float32)

    def panel(index, nothing):
        b = index // steps
        inner = pl.multiple_of(index % steps * width, width)

        def block(m, carry):
            most, least = carry
            total = None
            for tap in range(KW):
                start = pl.multiple_of((m * group + tap) * count, count)
                part = jnp.dot(
                    ext_ref[pl.ds(start, group * count), :],
                    conv_full[:, :, b, tap, :, pl.ds(inner, width)].reshape(channels, width),
                    preferred_element_type=jnp.float32,
                )
                total = part if total is None else total + part
            for piece_index in range(group):
                piece = total[piece_index * count : (piece_index + 1) * count]
                most = jnp.maximum(most, piece)
                least = jnp.minimum(least, piece)
            return most, least

        most, least = lax.fori_loop(0, POOL_B // group, block, (-big, big))
        at = pl.multiple_of(index * width, width)
        bias = conv_bias_ref[:, pl.ds(at, width)]
        coarse_ref[:, pl.ds(at, width)] = jnp.maximum(
            jax.nn.gelu(most + bias), jax.nn.gelu(least + bias)
        ).astype(jnp.bfloat16)
        return nothing

    panels = column_parts * steps
    early = panels // 2
    lax.fori_loop(0, early, panel, 0)
    third(1)
    lax.fori_loop(early, panels, panel, 0)
    fourth(1)
    finish(1)
    split = HEADS * HEAD_K
    middle = split + HEAD_K

    def weight(begin, end):
        return attn_full[:, :, :, begin:end].reshape(wide, end - begin)

    def turned(head):
        return (
            head * cosine_ref[...] + pltpu.roll(head, HEAD_K // 2, 1) * sine_ref[...]
        ).astype(jnp.bfloat16)

    hidden = rms_scale(coarse_ref[...].astype(jnp.float32), attn_gain_ref[...]).astype(
        jnp.bfloat16
    )
    key_ref[place] = turned(
        jnp.dot(hidden, weight(split, middle), preferred_element_type=jnp.float32)
    )
    value_ref[place] = jnp.dot(
        hidden, weight(middle + wide, middle + wide + HEAD_V), preferred_element_type=jnp.float32
    ).astype(jnp.bfloat16)
    pairs = []
    for turn in range(1, members):
        for index, ref in enumerate((key_ref, value_ref)):
            copy = pltpu.make_async_remote_copy(
                ref.at[place],
                ref.at[place],
                pair_send.at[index, turn],
                pair_recv.at[index, place],
                (me, (place + turn) % members),
                MESH,
            )
            copy.start()
            pairs.append(copy)
    query = jnp.dot(hidden, weight(0, split), preferred_element_type=jnp.float32)
    for turn in range(1, members):
        spot = (place + turn) % members
        for index, ref in enumerate((key_ref, value_ref)):
            pltpu.make_async_remote_copy(
                ref.at[spot],
                ref.at[spot],
                pair_send.at[index, 0],
                pair_recv.at[index, spot],
                (partner, place),
                MESH,
            ).wait_recv()
    keys = key_ref[...].reshape(members * count, HEAD_K)
    values = value_ref[...].reshape(members * count, HEAD_V)
    projection = weight(middle, middle + wide)
    total = coarse_ref[...].astype(jnp.float32)
    for head in range(HEADS):
        scores = lax.dot_general(
            turned(query[:, head * HEAD_K : (head + 1) * HEAD_K]),
            keys,
            (((1,), (1,)), ((), ())),
            preferred_element_type=jnp.float32,
        ) * HEAD_K ** (-0.5)
        raised = jnp.exp(scores - jnp.max(scores, axis=-1, keepdims=True))
        weights = (raised / jnp.sum(raised, axis=-1, keepdims=True)).astype(jnp.bfloat16)
        mixed = jnp.dot(weights, values, preferred_element_type=jnp.float32).astype(jnp.bfloat16)
        total = total + jnp.dot(
            mixed,
            projection[head * HEAD_V : (head + 1) * HEAD_V],
            preferred_element_type=jnp.float32,
        )
    out_ref[...] = total.astype(jnp.bfloat16)
    for copy in pairs:
        copy.wait_send()


def row_parts_of(depth, columns, members):
    for row_parts in (2, 1, 3):
        column_parts = members // row_parts
        if members % row_parts or depth % (16 * row_parts) or columns % (256 * column_parts):
            continue
        return row_parts, column_parts
    return None


def encoder_stage(tokens, stem_weight, vectors, cosine, sine, conv_weight, attn_rows, parts):
    count = tokens.shape[0]
    channels = stem_weight.shape[1]
    taps, depth, columns = conv_weight.shape
    ways = lax.axis_size("dp")
    members = lax.axis_size("seq")
    row_parts, column_parts = parts
    copies = (ways // 2 - 1) * (2 * members) + members + ways
    full_attn = (ways,) + attn_rows.shape
    vmem = pl.BlockSpec(memory_space=pltpu.VMEM)
    hbm = pl.BlockSpec(memory_space=pl.ANY)
    return pl.pallas_call(
        encoder_kernel,
        out_shape=jax.ShapeDtypeStruct((count, columns), jnp.bfloat16),
        in_specs=[vmem] * 5 + [hbm] * 2,
        out_specs=vmem,
        scratch_shapes=[
            pltpu.VMEM((count, columns), jnp.bfloat16),
            pltpu.VMEM((members, count, HEAD_K), jnp.bfloat16),
            pltpu.VMEM((members, count, HEAD_V), jnp.bfloat16),
            pltpu.SemaphoreType.DMA((2, members)),
            pltpu.SemaphoreType.DMA((2, members)),
            pltpu.VMEM((GROUP + 2 * SPAN, count), jnp.float32),
            pltpu.VMEM((POOL_B + 1, count, GROUP), jnp.bfloat16),
            pltpu.VMEM((POOL_A, GROUP, channels), jnp.bfloat16),
            pltpu.VMEM((count, channels), jnp.float32),
            pltpu.VMEM(((POOL_B + 4) * count, channels), jnp.bfloat16),
            pltpu.VMEM((8, GROUP), jnp.int32),
            pltpu.VMEM((8, GROUP), jnp.int32),
            pltpu.VMEM(
                (ways, row_parts, column_parts, taps, depth // row_parts, columns // column_parts),
                jnp.bfloat16,
            ),
            pltpu.VMEM(full_attn, jnp.bfloat16),
            pltpu.SemaphoreType.DMA((2,)),
            pltpu.SemaphoreType.DMA((2,)),
            pltpu.SemaphoreType.DMA((2, copies)),
            pltpu.SemaphoreType.DMA((2, ways, members)),
            pltpu.SemaphoreType.DMA((2, ways, 2)),
            pltpu.SemaphoreType.DMA((2, members)),
        ],
        compiler_params=pltpu.CompilerParams(
            collective_id=0, has_side_effects=True, vmem_limit_bytes=56 * 2**20
        ),
        name="encoder_stage",
    )(tokens, stem_weight, vectors[None], cosine, sine, conv_weight, attn_rows)


def gather_conv(conv_weight):
    taps, depth, columns = conv_weight.shape
    members = lax.axis_size("seq")
    place = lax.axis_index("seq")
    for row_parts in (2, 1, 3):
        column_parts = members // row_parts
        if members % row_parts or depth % (16 * row_parts) or columns % (256 * column_parts):
            continue
        depth_part = depth // row_parts
        column_part = columns // column_parts
        piece = lax.dynamic_slice(
            conv_weight,
            (0, place // column_parts * depth_part, place % column_parts * column_part),
            (taps, depth_part, column_part),
        )
        full = lax.all_gather(piece, ("dp", "seq"), axis=0, tiled=False)
        return full.reshape(-1, row_parts, column_parts, taps, depth_part, column_part)
    full = lax.all_gather(conv_weight, "dp", axis=0, tiled=False)
    return full[:, None, None]


def gather_rows(weight):
    members = lax.axis_size("seq")
    rows = weight.shape[0] // members
    piece = lax.dynamic_slice_in_dim(weight, lax.axis_index("seq") * rows, rows, axis=0)
    return lax.all_gather(piece, ("dp", "seq"), axis=0, tiled=True)


def body(
    tokens,
    stem_weight,
    stem_bias,
    conv_gain,
    conv_weight,
    conv_bias,
    attn_gain,
    w_query,
    w_key,
    w_value,
    w_out,
):
    seq_local = tokens.shape[1]
    rows_att = seq_local // GROUP
    tokens = tokens.reshape(rows_att, GROUP)
    size = lax.axis_size("seq")
    rows = w_out.shape[0]
    parts = row_parts_of(conv_weight.shape[1], conv_weight.shape[2], size)
    split = HEADS * HEAD_K
    if size == 4 and parts is not None and rows % (16 * size) == 0:
        packed = jnp.concatenate([w_query, w_key, w_out, w_value], axis=1)
        half_dim = HEAD_K // 2
        freqs = 10000.0 ** (-jnp.arange(half_dim, dtype=jnp.float32) / half_dim)
        positions = lax.axis_index("seq") * rows_att + jnp.arange(rows_att, dtype=jnp.int32)
        angles = positions.astype(jnp.float32)[:, None] * freqs[None, :]
        cosine, sine = jnp.cos(angles), jnp.sin(angles)
        return encoder_stage(
            tokens,
            stem_weight,
            jnp.concatenate([stem_bias, conv_gain, conv_bias, attn_gain]),
            jnp.concatenate([cosine, cosine], axis=1),
            jnp.concatenate([-sine, sine], axis=1),
            conv_weight,
            packed.reshape(size, rows // size, -1),
            parts,
        )[None]
    else:
        full_conv = gather_conv(conv_weight)
        projections = gather_rows(jnp.concatenate([w_query, w_key, w_value], axis=1))
        first_rows = projections[:, : split + HEAD_K]
        value_rows = projections[:, split + HEAD_K :]
        full_out = gather_rows(w_out)
        forward = [(i, i + 1) for i in range(size - 1)]
        backward = [(i + 1, i) for i in range(size - 1)]
        low = lax.ppermute(tokens[-1:], "seq", forward)
        high = lax.ppermute(tokens[:1], "seq", backward)
        ext = stem_stage(tokens, low, high, stem_weight, stem_bias, conv_gain)
        coarse = conv_stage(ext, full_conv, conv_bias)
    residual = coarse.astype(jnp.float32)
    hidden = rms_scale(residual, attn_gain).astype(jnp.bfloat16)
    projected = jnp.dot(hidden, first_rows, preferred_element_type=jnp.float32)
    query = projected[:, :split]
    keys = projected[:, split:]
    values = jnp.dot(hidden, value_rows, preferred_element_type=jnp.float32)
    half_dim = HEAD_K // 2
    freqs = 10000.0 ** (-jnp.arange(half_dim, dtype=jnp.float32) / half_dim)
    positions = lax.axis_index("seq") * rows_att + jnp.arange(rows_att, dtype=jnp.int32)
    angles = positions.astype(jnp.float32)[:, None] * freqs[None, :]
    query = rotate(query.reshape(rows_att, HEADS, HEAD_K), angles[:, None, :]).astype(jnp.bfloat16)
    keys = rotate(keys, angles).astype(jnp.bfloat16)
    pair = jnp.concatenate([keys, values.astype(jnp.bfloat16)], axis=1)
    pair = lax.all_gather(pair, "seq", axis=0, tiled=True)
    keys_all, values_all = pair[:, :HEAD_K], pair[:, HEAD_K:]
    scores = jnp.einsum(
        "rhd,kd->hrk", query, keys_all, preferred_element_type=jnp.float32
    ) * HEAD_K ** (-0.5)
    weights = jax.nn.softmax(scores, axis=-1).astype(jnp.bfloat16)
    mixed = jnp.einsum(
        "hrk,kd->rhd", weights, values_all, preferred_element_type=jnp.float32
    ).astype(jnp.bfloat16)
    mixed = mixed.reshape(rows_att, HEADS * HEAD_V)
    out = jnp.dot(mixed, full_out, preferred_element_type=jnp.float32)
    return (residual + out).astype(jnp.bfloat16)[None]


def solution(mesh):
    in_specs = (
        P("dp", "seq"),
        P(),
        P(),
        P(),
        P(None, "dp", None),
        P(),
        P(),
        P("dp", None),
        P("dp", None),
        P("dp", None),
        P("dp", None),
    )
    out_specs = P("dp", "seq", None)
    return jax.shard_map(body, mesh=mesh, in_specs=in_specs, out_specs=out_specs, check_vma=False)
```

profile of v0, /device:TPU:9, one launch (start us, length us, event | category | flops | bytes accessed | tf_op | source)
XLA Modules:
  0.0 130.1 jit_solution(8259345763683312693)
XLA Ops:
  0.0 0.7 pad_maximum_fusion.3
  0.8 0.6 broadcast_in_dim.8.vector_ref
  1.4 0.3 fusion
  1.7 0.7 pad_maximum_fusion.1
  2.4 2.3 %pad_maximum_fusion = bf16[192,2880]{1,0:T(8,128)(2,1)} fusion(bf16[192,192]{1,0:T(8,128)(2,1)} %param.20, bf16[192,1536]{1,0:T(8,128)(2,1)} %param.21, bf16[192,128]{1,0:T(8,128)(2,1)} %param.19, bf16[192,1024]{1,0:T(8,128)(2,1)} %param.18), kind=kLoop, calls=%fused_computation | loop fusion | flops 4423680 | bytes 2211840 | tf_op jit(solution)/shard_map/concatenate | solution.py:664
  4.8 123.6 %encoder_stage.1 = bf16[128,1536]{1,0:T(8,128)(2,1)} custom-call(s32[128,128]{1,0:T(8,128)} %bitcast.5, bf16[60,768]{1,0:T(8,128)(2,1)} %stem_weight_ref.1, f32[1,4608]{1,0:T(1,128)} %broadcast_in_dim.8.vector_ref, f32[128,128]{1,0:T(8,128)} %get-tuple-element.8.cosine_ref, f32[128,128]{1,0:T(8,128)} %get-tuple-element.9.sine_ref, ...), custom_call_target="tpu_custom_call" | custom-call | tf_op jit(solution)/shard_map/encoder_stage/pallas_call | solution.py:578
  128.4 1.8 %copy.13 = bf16[1,128,1536]{2,1,0:T(8,128)(2,1)} copy(bf16[1,128,1536]{2,1,0:T(8,128)(2,1)} %bitcast.4) | data formatting | bytes 786432
  (2 shorter events, 0.0 us)
where the time goes:
time: 130 us
  Pallas kernels  124 us (95%)
  other arithmetic  4.15 us (3%)
  local copies, waits for them, and re-layouts  2.38 us (2%)
    pallas_call x1, Pallas kernels, encoder_stage(): pl.pallas_call(encoder_kernel, out_shape=jax.ShapeDtypeStruct((count, col...  124 us

commit v1 on v0

v1 whole, which is shorter than its diff:
```python
import functools

import jax
import jax.numpy as jnp
from jax import lax
from jax.experimental import pallas as pl
from jax.experimental.pallas import tpu as pltpu
from jax.sharding import PartitionSpec as P

HEADS = 8
HEAD_K = 128
HEAD_V = 192
KW_STEM = 15
KW = 5
POOL_A = 8
POOL_B = 16
GROUP = POOL_A * POOL_B
SPAN = 24

epsilon = 1e-06


def rms_scale(values, gain):
    return values * lax.rsqrt(jnp.mean(values * values, axis=-1, keepdims=True) + epsilon) * gain


def rotate(values, angles):
    half_dim = values.shape[-1] // 2
    first = values[..., :half_dim]
    second = values[..., half_dim:]
    cosine = jnp.cos(angles)
    sine = jnp.sin(angles)
    return jnp.concatenate(
        [first * cosine - second * sine, second * cosine + first * sine], axis=-1
    )


def stem_kernel(
    tok_ref, low_ref, high_ref, weight_ref, bias_ref, gain_ref, ext_ref, text_ref, hot_ref, shifted_ref, rows_ref
):
    stem_compute(
        tok_ref,
        low_ref[...],
        high_ref[...],
        weight_ref,
        bias_ref,
        gain_ref,
        ext_ref,
        text_ref,
        hot_ref,
        shifted_ref,
        rows_ref,
    )


def stem_shift(weight_ref, shifted_ref):
    source = lax.broadcasted_iota(jnp.int32, (GROUP, weight_ref.shape[0]), 1)
    target = lax.broadcasted_iota(jnp.int32, (GROUP, weight_ref.shape[0]), 0)
    tap = source // 4
    base = source - 4 * tap
    for offset in range(POOL_A):
        pick = (target == base * SPAN + offset + tap + 1).astype(jnp.float32).astype(jnp.bfloat16)
        shifted_ref[offset] = jnp.dot(
            pick, weight_ref[...], preferred_element_type=jnp.float32
        ).astype(jnp.bfloat16)


def stem_tokens(tok_ref, low, high, text_ref, hot_ref):
    count = tok_ref.shape[0]
    main = tok_ref[...].astype(jnp.float32)
    row = lax.broadcasted_iota(jnp.int32, main.shape, 0)
    previous = jnp.where(row == 0, low.astype(jnp.float32), pltpu.roll(main, 1, 0))
    following = jnp.where(
        row == count - 1, high.astype(jnp.float32), pltpu.roll(main, count - 1, 0)
    )
    text_ref[0:SPAN, :] = previous.T[GROUP - SPAN :, :]
    text_ref[SPAN : SPAN + GROUP, :] = main.T
    text_ref[SPAN + GROUP :, :] = following.T[:SPAN, :]

    def hot_of(span):
        planes = [(span == float(code)).astype(jnp.float32) for code in range(1, 5)]
        planes.append(jnp.zeros((GROUP - 4 * SPAN, span.shape[1]), jnp.float32))
        return jnp.concatenate(planes, axis=0).T.astype(jnp.bfloat16)

    for j in range(POOL_B):
        hot_ref[j] = hot_of(text_ref[8 * j + SPAN - 8 : 8 * j + 2 * SPAN - 8, :])
    lane = lax.broadcasted_iota(jnp.int32, (SPAN, count), 1)
    edge = jnp.where(
        lane == 0,
        text_ref[0:SPAN, :],
        jnp.where(
            lane == 1,
            pltpu.roll(text_ref[8 : 8 + SPAN, :], 1, 1),
            jnp.where(
                lane == 2,
                pltpu.roll(text_ref[GROUP + SPAN - 8 : GROUP + 2 * SPAN - 8, :], 3, 1),
                pltpu.roll(text_ref[GROUP + SPAN : GROUP + 2 * SPAN, :], 4, 1),
            ),
        ),
    )
    hot_ref[POOL_B] = hot_of(edge)


def stem_block(j, bias_ref, gain_ref, ext_ref, hot_ref, shifted_ref, rows_ref):
    count, channels = rows_ref.shape
    width = 256
    hot = hot_ref[j]
    for chunk in range(channels // width):
        columns = slice(chunk * width, (chunk + 1) * width)
        best = None
        for offset in range(POOL_A):
            stem = jnp.dot(hot, shifted_ref[offset, :, columns], preferred_element_type=jnp.float32)
            best = stem if best is None else jnp.maximum(best, stem)
        pooled = jax.nn.gelu(best + bias_ref[:, columns]).astype(jnp.bfloat16)
        rows_ref[:, columns] = pooled.astype(jnp.float32)
    pooled = rows_ref[...]
    start = pl.multiple_of((j + 2) * count, count)
    ext_ref[pl.ds(start, count), :] = rms_scale(pooled, gain_ref[...]).astype(jnp.bfloat16)


def stem_edges(place, last_place, ext_ref, rows_ref):
    count, channels = rows_ref.shape
    edges = ext_ref[(POOL_B + 2) * count : (POOL_B + 3) * count, :].astype(jnp.float32)
    left_keep = (place > 0).astype(jnp.float32)
    right_keep = (place < last_place).astype(jnp.float32)
    spot = lax.broadcasted_iota(jnp.int32, (count, channels), 0)
    for index in range(2):
        inner = ext_ref[(POOL_B + index) * count : (POOL_B + index + 1) * count, :]
        moved = pltpu.roll(inner.astype(jnp.float32), 1, 0)
        ext_ref[index * count : (index + 1) * count, :] = jnp.where(
            spot == 0, edges[index : index + 1, :] * left_keep, moved
        ).astype(jnp.bfloat16)
        inner = ext_ref[(2 + index) * count : (3 + index) * count, :]
        moved = pltpu.roll(inner.astype(jnp.float32), count - 1, 0)
        at = POOL_B + 2 + index
        ext_ref[at * count : (at + 1) * count, :] = jnp.where(
            spot == count - 1, edges[2 + index : 3 + index, :] * right_keep, moved
        ).astype(jnp.bfloat16)


def stem_compute(
    tok_ref, low, high, weight_ref, bias_ref, gain_ref, ext_ref, text_ref, hot_ref, shifted_ref, rows_ref
):
    stem_shift(weight_ref, shifted_ref)
    stem_tokens(tok_ref, low, high, text_ref, hot_ref)

    def block(j, carry):
        stem_block(j, bias_ref, gain_ref, ext_ref, hot_ref, shifted_ref, rows_ref)
        return carry

    lax.fori_loop(0, POOL_B + 1, block, 0)
    stem_edges(lax.axis_index("seq"), lax.axis_size("seq") - 1, ext_ref, rows_ref)


def stem_stage(tokens, low, high, stem_weight, stem_bias, conv_gain):
    count = tokens.shape[0]
    channels = stem_weight.shape[1]
    return pl.pallas_call(
        stem_kernel,
        out_shape=jax.ShapeDtypeStruct(((POOL_B + 4) * count, channels), jnp.bfloat16),
        in_specs=[pl.BlockSpec(memory_space=pltpu.VMEM)] * 6,
        out_specs=pl.BlockSpec(memory_space=pltpu.VMEM),
        scratch_shapes=[
            pltpu.VMEM((GROUP + 2 * SPAN, count), jnp.float32),
            pltpu.VMEM((POOL_B + 1, count, GROUP), jnp.bfloat16),
            pltpu.VMEM((POOL_A, GROUP, channels), jnp.bfloat16),
            pltpu.VMEM((count, channels), jnp.float32),
        ],
        cost_estimate=pl.CostEstimate(
            flops=20_000_000_000, bytes_accessed=4_000_000, transcendentals=1_600_000
        ),
        name="stem_stage",
    )(tokens, low, high, stem_weight, stem_bias[None], conv_gain[None])


def conv_kernel(count, ext_ref, weight_ref, bias_ref, coarse_ref):
    group = 4
    width = weight_ref.shape[-1]
    channels = ext_ref.shape[1]

    def block(m, carry):
        most, least = carry
        total = None
        for tap in range(KW):
            start = pl.multiple_of((m * group + tap) * count, count)
            part = jnp.dot(
                ext_ref[pl.ds(start, group * count), :],
                weight_ref[:, :, 0, tap].reshape(channels, width),
                preferred_element_type=jnp.float32,
            )
            total = part if total is None else total + part
        for index in range(group):
            piece = total[index * count : (index + 1) * count]
            most = jnp.maximum(most, piece)
            least = jnp.minimum(least, piece)
        return most, least

    big = jnp.full((count, width), jnp.finfo(jnp.float32).max, jnp.float32)
    most, least = lax.fori_loop(0, POOL_B // group, block, (-big, big))
    bias = bias_ref[...]
    coarse_ref[...] = jnp.maximum(jax.nn.gelu(most + bias), jax.nn.gelu(least + bias)).astype(
        jnp.bfloat16
    )


def conv_stage(ext, weight, conv_bias):
    count = ext.shape[0] // (POOL_B + 4)
    ways, row_parts, column_parts, taps, depth, columns = weight.shape
    width = 256
    steps = columns // width
    return pl.pallas_call(
        functools.partial(conv_kernel, count),
        grid=(column_parts, steps),
        out_shape=jax.ShapeDtypeStruct((count, column_parts * columns), jnp.bfloat16),
        in_specs=[
            pl.BlockSpec(ext.shape, lambda b, n: (0, 0), pipeline_mode=pl.Buffered(1)),
            pl.BlockSpec(
                (ways, row_parts, 1, taps, depth, width), lambda b, n: (0, 0, b, 0, 0, n)
            ),
            pl.BlockSpec((1, width), lambda b, n: (0, b * steps + n)),
        ],
        out_specs=pl.BlockSpec((count, width), lambda b, n: (0, b * steps + n)),
        cost_estimate=pl.CostEstimate(
            flops=24_000_000_000, bytes_accessed=16_000_000, transcendentals=400_000
        ),
        name="conv_stage",
    )(ext, weight, conv_bias[None])


MESH = pl.DeviceIdType.MESH


UNITS = 12


def encoder_kernel(
    tok_ref,
    stem_weight_ref,
    stem_bias_ref,
    gain_ref,
    conv_bias_ref,
    attn_gain_ref,
    cosine_ref,
    sine_ref,
    conv_ref,
    query_ref,
    keyw_ref,
    valuew_ref,
    outw_ref,
    out_ref,
    coarse_ref,
    key_ref,
    value_ref,
    text_ref,
    hot_ref,
    shifted_ref,
    rows_ref,
    ext_ref,
    low_ref,
    high_ref,
    conv_full,
    proj_full,
    outw_full,
    pair_send,
    pair_recv,
    halo_send,
    halo_recv,
    local_sem,
    recv_sem,
    panel_sem,
    partner_sem,
    x_sem,
    y_sem,
    partner_send,
    own_sem,
    relay_sem,
):
    wide = out_ref.shape[1]
    members = lax.axis_size("seq")
    me = lax.axis_index("dp")
    place = lax.axis_index("seq")
    chip = me // 2
    core = me % 2
    chips = lax.axis_size("dp") // 2
    partner = (chip * 2 + 1 - core, place)
    count = tok_ref.shape[0]
    depth = conv_full.shape[3]
    unit_cols = conv_full.shape[4]
    unit_rows = proj_full.shape[1] // UNITS
    split = HEADS * HEAD_K
    middle = split + HEAD_K

    along_x = place + 1 - 2 * (place % 2)
    along_y = place + 2 - 4 * (place // 2)
    across = 3 - place
    mine = (place % 2 + place // 2) % 2
    theirs = 1 - mine
    x_target = (me, along_x)
    y_target = (me, along_y)

    sources = (1 + chip % 2, (chip + 2) % chips, 3 - 3 * (chip % 2))
    inner = (chip > 0) & (chip < chips - 1)
    relays = (3 * (chip - 1), None, chips - 1 - chip)

    z_units = (2 * place, 2 * place + 1, 8 + 2 * mine, 9 + 2 * mine)
    x_out = (2 * place, 2 * place + 1, 2 * along_y + 1, 8 + 2 * mine)
    y_out = (2 * place, 2 * place + 1, 2 * along_x, 9 + 2 * mine)
    x_in = (2 * along_x, 2 * along_x + 1, 2 * across + 1, 8 + 2 * theirs)
    y_in = (2 * along_y, 2 * along_y + 1, 2 * across, 9 + 2 * theirs)

    def part(kind, way, unit, span):
        if kind == 0:
            return conv_full.at[way, pl.ds(unit, span)]
        full = proj_full if kind == 1 else outw_full
        return full.at[way, pl.ds(pl.multiple_of(unit * unit_rows, unit_rows), span * unit_rows)]

    def z_message(kind, i):
        return (z_units[i], 1) if kind == 0 else (z_units[2 * i], 2)

    def plane_messages(kind, i):
        if kind == 0:
            return ((i, 1),)
        return ((0, 2),) if i == 0 else ((2, 1), (3, 1))

    def remote(ref, send_sem, recv, target):
        return pltpu.make_async_remote_copy(ref, ref, send_sem, recv, target, MESH)

    def arrived(ref, recv):
        remote(ref, x_sem.at[0], recv, partner).wait_recv()

    def to_partner(kind, way, unit, span):
        recv = panel_sem.at[unit // 2] if kind == 0 else partner_sem.at[kind]
        remote(part(kind, way, unit, span), partner_send.at[kind], recv, partner).start()

    def own(kind, i):
        ref = part(kind, me, *z_message(kind, i))
        recv = recv_sem.at[kind, chip, i]

        @pl.when(chip < chips - 1)
        def _():
            remote(ref, own_sem.at[kind, 0], recv, (me + 2, place)).start()

        @pl.when(chip > 0)
        def _():
            remote(ref, own_sem.at[kind, 1], recv, (me - 2, place)).start()

        @pl.when(jnp.logical_not(inner))
        def _():
            far = 2 * (chips - 1 - chip) + core
            remote(ref, own_sem.at[kind, 2], recv, (far, place)).start()

    def z_step(kind, i, j):
        origin = sources[j]
        way = 2 * origin + core
        unit, span = z_message(kind, i)
        ref = part(kind, way, unit, span)
        recv = recv_sem.at[kind, origin, i]
        arrived(ref, recv)
        if relays[j] is not None:

            @pl.when(inner)
            def _():
                remote(ref, relay_sem.at[kind, j // 2], recv, (2 * relays[j] + core, place)).start()

        for k, width in plane_messages(kind, i):
            for base, units, sem, target in ((4, x_out, x_sem, x_target), (8, y_out, y_sem, y_target)):
                recv = recv_sem.at[kind, origin, base + k]
                remote(part(kind, way, units[k], width), sem.at[kind], recv, target).start()
        to_partner(kind, way, unit, span)

    def plane_step(kind, i, j):
        origin = sources[j]
        way = 2 * origin + core
        for k, width in plane_messages(kind, i):
            for base, units in ((4, x_in), (8, y_in)):
                arrived(part(kind, way, units[k], width), recv_sem.at[kind, origin, base + k])
                to_partner(kind, way, units[k], width)

    stream = ((0, 0), (0, 1), (0, 2), (0, 3), (1, 0), (1, 1), (2, 0), (2, 1))
    events = []
    for turn in range(len(stream) + 1):
        for j in range(3):
            at = turn - (j == 1)
            if 0 <= at < len(stream) and not (turn == len(stream) and j != 1):
                events.append((at, j))
    lag = 2

    def event(n):
        def plane():
            if lag <= n < len(events) + lag:
                at, j = events[n - lag]
                plane_step(*stream[at], j)

        last = n == len(events) - 1
        if last:
            plane()
        if n < len(events):
            at, j = events[n]
            z_step(*stream[at], j)
            if j == 2 and at + 2 < len(stream):
                own(*stream[at + 2])
        if not last:
            plane()

    def event_of(number, first, last):
        for n in range(first, last):

            @pl.when(number == n - first)
            def _():
                event(n)

    def local_copies(kind):
        if kind == 0:
            for unit in range(UNITS):
                yield conv_ref.at[:, :, pl.ds(unit * unit_cols, unit_cols)], conv_full.at[me, unit]
        elif kind == 1:
            yield query_ref, proj_full.at[me, :, pl.ds(0, split)]
            yield keyw_ref, proj_full.at[me, :, pl.ds(split, HEAD_K)]
            yield valuew_ref, proj_full.at[me, :, pl.ds(middle, HEAD_V)]
        else:
            yield outw_ref, outw_full.at[me]

    def local_start(kind):
        for a, b in local_copies(kind):
            pltpu.make_async_copy(a, b, local_sem.at[kind]).start()

    def local_wait(kind):
        whole = (conv_full, proj_full, outw_full)[kind].at[me]
        pltpu.make_async_copy(whole, whole, local_sem.at[kind]).wait()

    def own_partner(kind):
        if kind == 0:
            for panel in range(UNITS // 2):
                to_partner(0, me, 2 * panel, 2)
        else:
            to_partner(kind, me, 0, UNITS)

    local_start(0)
    barrier = pltpu.get_barrier_semaphore()
    pl.semaphore_signal(barrier, inc=1, device_id=partner, device_id_type=MESH)
    for turn in range(1, members):
        pl.semaphore_signal(
            barrier, inc=1, device_id=(me, (place + turn) % members), device_id_type=MESH
        )

    for turn in (1, chips - 1):
        neighbour = (chip + turn) % chips * 2 + core
        pl.semaphore_signal(barrier, inc=1, device_id=(neighbour, place), device_id_type=MESH)
    local_start(1)
    local_start(2)
    local_wait(0)
    pl.semaphore_wait(barrier, members + 2)

    own(0, 0)
    own(0, 1)
    right = (place + 1) % members
    left = (place + members - 1) % members
    halo = [
        pltpu.make_async_remote_copy(
            tok_ref.at[count - 8 : count], low_ref, halo_send.at[0], halo_recv.at[0], (me, right), MESH
        ),
        pltpu.make_async_remote_copy(
            tok_ref.at[0:8], high_ref, halo_send.at[1], halo_recv.at[1], (me, left), MESH
        ),
    ]
    for copy in halo:
        copy.start()
    own_partner(0)
    local_wait(1)
    own_partner(1)
    local_wait(2)
    own_partner(2)
    stem_shift(stem_weight_ref, shifted_ref)
    for copy in halo:
        copy.wait()
    low = jnp.where(place > 0, low_ref[7:8], 0)
    high = jnp.where(place < members - 1, high_ref[0:1], 0)
    stem_tokens(tok_ref, low, high, text_ref, hot_ref)

    def stem_round(r, nothing):
        def block(j, nothing):
            stem_block(j, stem_bias_ref, gain_ref, ext_ref, hot_ref, shifted_ref, rows_ref)
            return nothing

        lax.fori_loop(3 * r - (r + 5) // 6, 3 * r + 2, block, 0)
        event_of(r, 0, 6)
        return nothing

    lax.fori_loop(0, (POOL_B + 2) // 3, stem_round, 0)
    stem_edges(place, members - 1, ext_ref, rows_ref)
    event(6)

    width = 2 * unit_cols
    group = 8
    channels = ext_ref.shape[1]
    big = jnp.full((count, width), jnp.finfo(jnp.float32).max, jnp.float32)

    def conv_panel(panel, after):
        block_of = pl.ds(0, chips)
        whole = conv_full.at[block_of, pl.ds(0, 2)]
        arrived(whole, panel_sem.at[panel])

        def block(m, carry):
            most, least = carry
            total = None
            for tap in range(KW):
                start = pl.multiple_of((m * group + tap) * count, count)
                weight = jnp.concatenate(
                    [conv_full[:, 2 * panel + h, tap].reshape(channels, unit_cols) for h in range(2)], axis=1
                )
                piece = jnp.dot(
                    ext_ref[pl.ds(start, group * count), :], weight, preferred_element_type=jnp.float32
                )
                total = piece if total is None else total + piece
            for index in range(group):
                piece = total[index * count : (index + 1) * count]
                most = jnp.maximum(most, piece)
                least = jnp.minimum(least, piece)
            after(m)
            return most, least

        most, least = lax.fori_loop(0, POOL_B // group, block, (-big, big))
        at = pl.multiple_of(panel * width, width)
        bias = conv_bias_ref[:, pl.ds(at, width)]
        coarse_ref[:, pl.ds(at, width)] = jnp.maximum(
            jax.nn.gelu(most + bias), jax.nn.gelu(least + bias)
        ).astype(jnp.bfloat16)

    def conv_turn(t, nothing):
        plane = (place % 2 + t % 2) % 2 + 2 * ((place // 2 + t // 2) % 2)
        shared = t // 4
        panel = (1 - shared) * plane + shared * (4 + (mine + t) % 2)
        conv_panel(panel, lambda m: event_of(2 * t + m, 7, 19))
        return nothing

    lax.fori_loop(0, UNITS // 2, conv_turn, 0)
    event(19)
    event(20)
    arrived(proj_full.at[pl.ds(0, chips)], partner_sem.at[1])

    def weight(begin, end):
        return proj_full[:, :, begin:end].reshape(wide, end - begin)

    cosine = jnp.concatenate([cosine_ref[...], cosine_ref[...]], axis=1)
    sine = jnp.concatenate([-sine_ref[...], sine_ref[...]], axis=1)

    def turned(head):
        return (head * cosine + pltpu.roll(head, HEAD_K // 2, 1) * sine).astype(jnp.bfloat16)

    hidden = rms_scale(coarse_ref[...].astype(jnp.float32), attn_gain_ref[...]).astype(
        jnp.bfloat16
    )
    key_ref[place] = turned(
        jnp.dot(hidden, weight(split, middle), preferred_element_type=jnp.float32)
    )
    value_ref[place] = jnp.dot(
        hidden, weight(middle, middle + HEAD_V), preferred_element_type=jnp.float32
    ).astype(jnp.bfloat16)
    pairs = []
    for turn in range(1, members):
        for index, ref in enumerate((key_ref, value_ref)):
            copy = pltpu.make_async_remote_copy(
                ref.at[place],
                ref.at[place],
                pair_send.at[index, turn],
                pair_recv.at[index, place],
                (me, (place + turn) % members),
                MESH,
            )
            copy.start()
            pairs.append(copy)
    query = jnp.dot(hidden, weight(0, split), preferred_element_type=jnp.float32)
    event(21)
    for turn in range(1, members):
        spot = (place + turn) % members
        for index, ref in enumerate((key_ref, value_ref)):
            arrived(ref.at[spot], pair_recv.at[index, spot])
    keys = key_ref[...].reshape(members * count, HEAD_K)
    values = value_ref[...].reshape(members * count, HEAD_V)
    mixes = []
    for head in range(HEADS):
        scores = lax.dot_general(
            turned(query[:, head * HEAD_K : (head + 1) * HEAD_K]),
            keys,
            (((1,), (1,)), ((), ())),
            preferred_element_type=jnp.float32,
        ) * HEAD_K ** (-0.5)
        raised = jnp.exp(scores - jnp.max(scores, axis=-1, keepdims=True))
        weights = (raised / jnp.sum(raised, axis=-1, keepdims=True)).astype(jnp.bfloat16)
        mixes.append(
            jnp.dot(weights, values, preferred_element_type=jnp.float32).astype(jnp.bfloat16)
        )
        if head in (3, 7):
            event(22 + head // 4)
    for n in range(24, len(events) + lag):
        event(n)
    arrived(outw_full.at[pl.ds(0, chips)], partner_sem.at[2])
    total = coarse_ref[...].astype(jnp.float32)
    for head in range(HEADS):
        total = total + jnp.dot(mixes[head], outw_full[head], preferred_element_type=jnp.float32)
    out_ref[...] = total.astype(jnp.bfloat16)
    for copy in pairs:
        copy.wait_send()
    for kind, full in enumerate((conv_full, proj_full, outw_full)):
        whole = full.at[0]
        remote(whole, x_sem.at[kind], recv_sem.at[0, 0, 0], x_target).wait_send()
        remote(whole, y_sem.at[kind], recv_sem.at[0, 0, 0], y_target).wait_send()
        every = full.at[pl.ds(0, chips)]
        remote(every, partner_send.at[kind], recv_sem.at[0, 0, 0], partner).wait_send()
        ref = part(kind, 0, 0, 4)

        @pl.when(chip < chips - 1)
        def _():
            remote(ref, own_sem.at[kind, 0], recv_sem.at[0, 0, 0], partner).wait_send()

        @pl.when(chip > 0)
        def _():
            remote(ref, own_sem.at[kind, 1], recv_sem.at[0, 0, 0], partner).wait_send()

        @pl.when(jnp.logical_not(inner))
        def _():
            remote(ref, own_sem.at[kind, 2], recv_sem.at[0, 0, 0], partner).wait_send()

        @pl.when(inner)
        def _():
            for index in range(2):
                remote(ref, relay_sem.at[kind, index], recv_sem.at[0, 0, 0], partner).wait_send()


def fits(ways, members, conv_weight, w_query, w_out):
    taps, depth, columns = conv_weight.shape
    rows = w_out.shape[0]
    return (
        ways == 8
        and members == 4
        and columns == UNITS * 128
        and depth % 16 == 0
        and rows == HEAD_V
        and HEADS == ways
        and rows % (16 * UNITS) == 0
    )


def encoder_stage(
    tokens, stem_weight, vectors, cosine, sine, conv_weight, w_query, w_key, w_value, w_out
):
    count = tokens.shape[0]
    channels = stem_weight.shape[1]
    taps, depth, columns = conv_weight.shape
    rows = w_out.shape[0]
    ways = lax.axis_size("dp")
    members = lax.axis_size("seq")
    chips = ways // 2
    vmem = pl.BlockSpec(memory_space=pltpu.VMEM)
    hbm = pl.BlockSpec(memory_space=pl.ANY)
    dma = pltpu.SemaphoreType.DMA
    return pl.pallas_call(
        encoder_kernel,
        out_shape=jax.ShapeDtypeStruct((count, columns), jnp.bfloat16),
        in_specs=[vmem] * 8 + [hbm] * 5,
        out_specs=vmem,
        scratch_shapes=[
            pltpu.VMEM((count, columns), jnp.bfloat16),
            pltpu.VMEM((members, count, HEAD_K), jnp.bfloat16),
            pltpu.VMEM((members, count, HEAD_V), jnp.bfloat16),
            pltpu.VMEM((GROUP + 2 * SPAN, count), jnp.float32),
            pltpu.VMEM((POOL_B + 1, count, GROUP), jnp.bfloat16),
            pltpu.VMEM((POOL_A, GROUP, channels), jnp.bfloat16),
            pltpu.VMEM((count, channels), jnp.float32),
            pltpu.VMEM(((POOL_B + 4) * count, channels), jnp.bfloat16),
            pltpu.VMEM((8, GROUP), jnp.int32),
            pltpu.VMEM((8, GROUP), jnp.int32),
            pltpu.VMEM((ways, UNITS, taps, depth, columns // UNITS), jnp.bfloat16),
            pltpu.VMEM((ways, rows, HEADS * HEAD_K + HEAD_K + HEAD_V), jnp.bfloat16),
            pltpu.VMEM((ways, rows, columns), jnp.bfloat16),
            dma((2, members)),
            dma((2, members)),
            dma((2,)),
            dma((2,)),
            dma((3,)),
            dma((3, chips, UNITS)),
            dma((UNITS // 2,)),
            dma((3,)),
            dma((3,)),
            dma((3,)),
            dma((3,)),
            dma((3, 3)),
            dma((3, 2)),
        ],
        compiler_params=pltpu.CompilerParams(
            collective_id=0, has_side_effects=True, vmem_limit_bytes=56 * 2**20
        ),
        name="encoder_stage",
    )(tokens, stem_weight, *vectors, cosine, sine, conv_weight, w_query, w_key, w_value, w_out)


def gather_conv(conv_weight):
    taps, depth, columns = conv_weight.shape
    members = lax.axis_size("seq")
    place = lax.axis_index("seq")
    for row_parts in (2, 1, 3):
        column_parts = members // row_parts
        if members % row_parts or depth % (16 * row_parts) or columns % (256 * column_parts):
            continue
        depth_part = depth // row_parts
        column_part = columns // column_parts
        piece = lax.dynamic_slice(
            conv_weight,
            (0, place // column_parts * depth_part, place % column_parts * column_part),
            (taps, depth_part, column_part),
        )
        full = lax.all_gather(piece, ("dp", "seq"), axis=0, tiled=False)
        return full.reshape(-1, row_parts, column_parts, taps, depth_part, column_part)
    full = lax.all_gather(conv_weight, "dp", axis=0, tiled=False)
    return full[:, None, None]


def gather_rows(weight):
    members = lax.axis_size("seq")
    rows = weight.shape[0] // members
    piece = lax.dynamic_slice_in_dim(weight, lax.axis_index("seq") * rows, rows, axis=0)
    return lax.all_gather(piece, ("dp", "seq"), axis=0, tiled=True)


def body(
    tokens,
    stem_weight,
    stem_bias,
    conv_gain,
    conv_weight,
    conv_bias,
    attn_gain,
    w_query,
    w_key,
    w_value,
    w_out,
):
    seq_local = tokens.shape[1]
    rows_att = seq_local // GROUP
    tokens = tokens.reshape(rows_att, GROUP)
    size = lax.axis_size("seq")
    rows = w_out.shape[0]
    split = HEADS * HEAD_K
    if fits(lax.axis_size("dp"), size, conv_weight, w_query, w_out):
        half_dim = HEAD_K // 2
        freqs = 10000.0 ** (-jnp.arange(half_dim, dtype=jnp.float32) / half_dim)
        positions = lax.axis_index("seq") * rows_att + jnp.arange(rows_att, dtype=jnp.int32)
        angles = positions.astype(jnp.float32)[:, None] * freqs[None, :]
        return encoder_stage(
            tokens,
            stem_weight,
            [vector[None] for vector in (stem_bias, conv_gain, conv_bias, attn_gain)],
            jnp.cos(angles),
            jnp.sin(angles),
            conv_weight,
            w_query,
            w_key,
            w_value,
            w_out,
        )[None]
    else:
        full_conv = gather_conv(conv_weight)
        projections = gather_rows(jnp.concatenate([w_query, w_key, w_value], axis=1))
        first_rows = projections[:, : split + HEAD_K]
        value_rows = projections[:, split + HEAD_K :]
        full_out = gather_rows(w_out)
        forward = [(i, i + 1) for i in range(size - 1)]
        backward = [(i + 1, i) for i in range(size - 1)]
        low = lax.ppermute(tokens[-1:], "seq", forward)
        high = lax.ppermute(tokens[:1], "seq", backward)
        ext = stem_stage(tokens, low, high, stem_weight, stem_bias, conv_gain)
        coarse = conv_stage(ext, full_conv, conv_bias)
    residual = coarse.astype(jnp.float32)
    hidden = rms_scale(residual, attn_gain).astype(jnp.bfloat16)
    projected = jnp.dot(hidden, first_rows, preferred_element_type=jnp.float32)
    query = projected[:, :split]
    keys = projected[:, split:]
    values = jnp.dot(hidden, value_rows, preferred_element_type=jnp.float32)
    half_dim = HEAD_K // 2
    freqs = 10000.0 ** (-jnp.arange(half_dim, dtype=jnp.float32) / half_dim)
    positions = lax.axis_index("seq") * rows_att + jnp.arange(rows_att, dtype=jnp.int32)
    angles = positions.astype(jnp.float32)[:, None] * freqs[None, :]
    query = rotate(query.reshape(rows_att, HEADS, HEAD_K), angles[:, None, :]).astype(jnp.bfloat16)
    keys = rotate(keys, angles).astype(jnp.bfloat16)
    pair = jnp.concatenate([keys, values.astype(jnp.bfloat16)], axis=1)
    pair = lax.all_gather(pair, "seq", axis=0, tiled=True)
    keys_all, values_all = pair[:, :HEAD_K], pair[:, HEAD_K:]
    scores = jnp.einsum(
        "rhd,kd->hrk", query, keys_all, preferred_element_type=jnp.float32
    ) * HEAD_K ** (-0.5)
    weights = jax.nn.softmax(scores, axis=-1).astype(jnp.bfloat16)
    mixed = jnp.einsum(
        "hrk,kd->rhd", weights, values_all, preferred_element_type=jnp.float32
    ).astype(jnp.bfloat16)
    mixed = mixed.reshape(rows_att, HEADS * HEAD_V)
    out = jnp.dot(mixed, full_out, preferred_element_type=jnp.float32)
    return (residual + out).astype(jnp.bfloat16)[None]


def solution(mesh):
    in_specs = (
        P("dp", "seq"),
        P(),
        P(),
        P(),
        P(None, "dp", None),
        P(),
        P(),
        P("dp", None),
        P("dp", None),
        P("dp", None),
        P("dp", None),
    )
    out_specs = P("dp", "seq", None)
    return jax.shard_map(body, mesh=mesh, in_specs=in_specs, out_specs=out_specs, check_vma=False)
```

time: 130 us -> 99.8 us (0.77)
  Pallas kernels: 124 us -> 91.6 us
  local copies, waits for them, and re-layouts: 2.38 us -> 6.91 us
  other arithmetic: 4.15 us -> 0.97 us
    pallas_call x1, Pallas kernels: 124 us -> 91.6 us  [encoder_stage(): pl.pallas_call(encoder_kernel, out_shape=jax.ShapeDtypeStruct((count, col...]
    broadcast_in_dim x1 -> x4, local copies, waits for them, and re-layouts: 0.61 us -> 5.14 us  [body(): vector[None]]
    concatenate x3 -> x0, other arithmetic: 3.83 us -> none  [the longest x1 2.33 us: body(): packed = jnp.concatenate([w_query, w_key, w_out, w_value], axis=1)]
where the time goes in v1:
time: 99.8 us; the launch traced here: 99.5 us
  Pallas kernels  91.6 us (92%)
  local copies, waits for them, and re-layouts  6.91 us (7%)
    pallas_call x1, Pallas kernels, encoder_stage(): pl.pallas_call(encoder_kernel, out_shape=jax.ShapeDtypeStruct((count, col...  91.6 us
    broadcast_in_dim x4, local copies, waits for them, and re-layouts, body(): vector[None]  5.14 us

profile of v1, /device:TPU:9, one launch (start us, length us, event | category | flops | bytes accessed | tf_op | source)
XLA Modules:
  0.0 99.5 jit_solution(15838793037407969430)
XLA Ops:
  0.0 1.3 %broadcast_in_dim.17.stem_bias_ref = f32[1,768]{1,0:T(1,128)} reshape(f32[768]{0:T(1024)} %param.13) | data formatting | bytes 6144 | tf_op jit(solution)/shard_map/broadcast_in_dim | solution.py:752
  1.3 1.3 %broadcast_in_dim.18.gain_ref = f32[1,768]{1,0:T(1,128)} reshape(f32[768]{0:T(1024)} %param.14) | data formatting | bytes 6144 | tf_op jit(solution)/shard_map/broadcast_in_dim | solution.py:752
  2.6 1.3 %broadcast_in_dim.19.conv_bias_ref = f32[1,1536]{1,0:T(1,128)} reshape(f32[1536]{0:T(1024)} %param.16) | data formatting | bytes 12288 | tf_op jit(solution)/shard_map/broadcast_in_dim | solution.py:752
  3.9 1.3 %broadcast_in_dim.20.attn_gain_ref = f32[1,1536]{1,0:T(1,128)} reshape(f32[1536]{0:T(1024)} %param.17) | data formatting | bytes 12288 | tf_op jit(solution)/shard_map/broadcast_in_dim | solution.py:752
  5.2 1.0 multiply_sine_fusion
  6.1 91.6 %encoder_stage.1 = bf16[128,1536]{1,0:T(8,128)(2,1)} custom-call(s32[128,128]{1,0:T(8,128)} %bitcast.3, bf16[60,768]{1,0:T(8,128)(2,1)} %stem_weight_ref.1, f32[1,768]{1,0:T(1,128)} %broadcast_in_dim.17.stem_bias_ref, f32[1,768]{1,0:T(1,128)} %broadcast_in_dim.18.gain_ref, f32[1,1536]{1,0:T(1,128)} %broadcast_in_dim.19.conv_bias_ref, ...), custom_call_target="tpu_custom_call" | custom-call | tf_op jit(solution)/shard_map/encoder_stage/pallas_call | solution.py:657
  97.7 1.8 %copy.13 = bf16[1,128,1536]{2,1,0:T(8,128)(2,1)} copy(bf16[1,128,1536]{2,1,0:T(8,128)(2,1)} %bitcast.2) | data formatting | bytes 786432
  (2 shorter events, 0.0 us)

commit v2 on v1

--- a/solution.py
+++ b/solution.py
@@ -1,4 +1,5 @@
 import functools
+import math
 
 import jax
 import jax.numpy as jnp
@@ -65,26 +66,31 @@
         ).astype(jnp.bfloat16)
 
 
-def stem_tokens(tok_ref, low, high, text_ref, hot_ref):
-    count = tok_ref.shape[0]
-    main = tok_ref[...].astype(jnp.float32)
-    row = lax.broadcasted_iota(jnp.int32, main.shape, 0)
-    previous = jnp.where(row == 0, low.astype(jnp.float32), pltpu.roll(main, 1, 0))
-    following = jnp.where(
-        row == count - 1, high.astype(jnp.float32), pltpu.roll(main, count - 1, 0)
-    )
-    text_ref[0:SPAN, :] = previous.T[GROUP - SPAN :, :]
-    text_ref[SPAN : SPAN + GROUP, :] = main.T
-    text_ref[SPAN + GROUP :, :] = following.T[:SPAN, :]
-
-    def hot_of(span):
-        planes = [(span == float(code)).astype(jnp.float32) for code in range(1, 5)]
-        planes.append(jnp.zeros((GROUP - 4 * SPAN, span.shape[1]), jnp.float32))
-        return jnp.concatenate(planes, axis=0).T.astype(jnp.bfloat16)
-
-    for j in range(POOL_B):
+def hot_of(span):
+    planes = [(span == float(code)).astype(jnp.float32) for code in range(1, 5)]
+    planes.append(jnp.zeros((GROUP - 4 * SPAN, span.shape[1]), jnp.float32))
+    return jnp.concatenate(planes, axis=0).T.astype(jnp.bfloat16)
+
+
+def stem_inside(tok_ref, text_ref, hot_ref):
+    text_ref[SPAN : SPAN + GROUP, :] = tok_ref[...].astype(jnp.float32).T
+    for j in range(1, POOL_B - 1):
         hot_ref[j] = hot_of(text_ref[8 * j + SPAN - 8 : 8 * j + 2 * SPAN - 8, :])
+
+
+def stem_outside(low, high, text_ref, hot_ref):
+    count = text_ref.shape[1]
     lane = lax.broadcasted_iota(jnp.int32, (SPAN, count), 1)
+    before = low.astype(jnp.float32)
+    after = high.astype(jnp.float32)
+    text_ref[0:SPAN, :] = jnp.where(
+        lane == 0, before[GROUP - SPAN :, :], pltpu.roll(text_ref[GROUP : GROUP + SPAN, :], 1, 1)
+    )
+    text_ref[SPAN + GROUP :, :] = jnp.where(
+        lane == count - 1, after[:SPAN, :], pltpu.roll(text_ref[SPAN : 2 * SPAN, :], count - 1, 1)
+    )
+    for j in (0, POOL_B - 1):
+        hot_ref[j] = hot_of(text_ref[8 * j + SPAN - 8 : 8 * j + 2 * SPAN - 8, :])
     edge = jnp.where(
         lane == 0,
         text_ref[0:SPAN, :],
@@ -101,6 +107,10 @@
     hot_ref[POOL_B] = hot_of(edge)
 
 
+def column_of(row, count):
+    return jnp.broadcast_to(row.astype(jnp.float32), (8, count)).T[:, 0:1]
+
+
 def stem_block(j, bias_ref, gain_ref, ext_ref, hot_ref, shifted_ref, rows_ref):
     count, channels = rows_ref.shape
     width = 256
@@ -111,11 +121,11 @@
         for offset in range(POOL_A):
             stem = jnp.dot(hot, shifted_ref[offset, :, columns], preferred_element_type=jnp.float32)
             best = stem if best is None else jnp.maximum(best, stem)
-        pooled = jax.nn.gelu(best + bias_ref[:, columns]).astype(jnp.bfloat16)
+        pooled = jax.nn.gelu(best + bias_ref[columns].reshape(1, width)).astype(jnp.bfloat16)
         rows_ref[:, columns] = pooled.astype(jnp.float32)
     pooled = rows_ref[...]
     start = pl.multiple_of((j + 2) * count, count)
-    ext_ref[pl.ds(start, count), :] = rms_scale(pooled, gain_ref[...]).astype(jnp.bfloat16)
+    ext_ref[pl.ds(start, count), :] = rms_scale(pooled, gain_ref[...].reshape(1, channels)).astype(jnp.bfloat16)
 
 
 def stem_edges(place, last_place, ext_ref, rows_ref):
@@ -142,7 +152,8 @@
     tok_ref, low, high, weight_ref, bias_ref, gain_ref, ext_ref, text_ref, hot_ref, shifted_ref, rows_ref
 ):
     stem_shift(weight_ref, shifted_ref)
-    stem_tokens(tok_ref, low, high, text_ref, hot_ref)
+    stem_inside(tok_ref, text_ref, hot_ref)
+    stem_outside(column_of(low, GROUP), column_of(high, GROUP), text_ref, hot_ref)
 
     def block(j, carry):
         stem_block(j, bias_ref, gain_ref, ext_ref, hot_ref, shifted_ref, rows_ref)
@@ -170,7 +181,7 @@
             flops=20_000_000_000, bytes_accessed=4_000_000, transcendentals=1_600_000
         ),
         name="stem_stage",
-    )(tokens, low, high, stem_weight, stem_bias[None], conv_gain[None])
+    )(tokens, low, high, stem_weight, stem_bias, conv_gain)
 
 
 def conv_kernel(count, ext_ref, weight_ref, bias_ref, coarse_ref):
@@ -231,6 +242,7 @@
 
 
 UNITS = 12
+GROUPS = 3
 
 
 def encoder_kernel(
@@ -240,8 +252,6 @@
     gain_ref,
     conv_bias_ref,
     attn_gain_ref,
-    cosine_ref,
-    sine_ref,
     conv_ref,
     query_ref,
     keyw_ref,
@@ -255,6 +265,7 @@
     hot_ref,
     shifted_ref,
     rows_ref,
+    turn_ref,
     ext_ref,
     low_ref,
     high_ref,
@@ -267,7 +278,6 @@
     halo_recv,
     local_sem,
     recv_sem,
-    panel_sem,
     partner_sem,
     x_sem,
     y_sem,
@@ -284,9 +294,9 @@
     chips = lax.axis_size("dp") // 2
     partner = (chip * 2 + 1 - core, place)
     count = tok_ref.shape[0]
-    depth = conv_full.shape[3]
-    unit_cols = conv_full.shape[4]
+    depth, width = conv_full.shape[5:]
     unit_rows = proj_full.shape[1] // UNITS
+    kinds = GROUPS + 2
     split = HEADS * HEAD_K
     middle = split + HEAD_K
 
@@ -302,25 +312,22 @@
     inner = (chip > 0) & (chip < chips - 1)
     relays = (3 * (chip - 1), None, chips - 1 - chip)
 
-    z_units = (2 * place, 2 * place + 1, 8 + 2 * mine, 9 + 2 * mine)
-    x_out = (2 * place, 2 * place + 1, 2 * along_y + 1, 8 + 2 * mine)
-    y_out = (2 * place, 2 * place + 1, 2 * along_x, 9 + 2 * mine)
-    x_in = (2 * along_x, 2 * along_x + 1, 2 * across + 1, 8 + 2 * theirs)
-    y_in = (2 * along_y, 2 * along_y + 1, 2 * across, 9 + 2 * theirs)
-
-    def part(kind, way, unit, span):
-        if kind == 0:
-            return conv_full.at[way, pl.ds(unit, span)]
-        full = proj_full if kind == 1 else outw_full
-        return full.at[way, pl.ds(pl.multiple_of(unit * unit_rows, unit_rows), span * unit_rows)]
-
-    def z_message(kind, i):
-        return (z_units[i], 1) if kind == 0 else (z_units[2 * i], 2)
-
-    def plane_messages(kind, i):
-        if kind == 0:
-            return ((i, 1),)
-        return ((0, 2),) if i == 0 else ((2, 1), (3, 1))
+    first = (place, 4 + mine)
+    x_out = ((0, place, None), (1, along_y, 1), (2, 4 + mine, 0))
+    y_out = ((0, place, None), (1, along_x, 0), (2, 4 + mine, 1))
+    x_in = ((0, along_x, None), (1, across, 1), (2, 4 + theirs, 0))
+    y_in = ((0, along_y, None), (1, across, 0), (2, 4 + theirs, 1))
+
+    def full_of(kind):
+        return (*(conv_full.at[group] for group in range(GROUPS)), proj_full, outw_full)[kind]
+
+    def part(kind, way, pair, half=None):
+        full = full_of(kind).at[way]
+        if kind < GROUPS:
+            return full.at[pair] if half is None else full.at[pair, half]
+        unit = 2 * pair + (half or 0)
+        span = 2 if half is None else 1
+        return full.at[pl.ds(pl.multiple_of(unit * unit_rows, unit_rows), span * unit_rows)]
 
     def remote(ref, send_sem, recv, target):
         return pltpu.make_async_remote_copy(ref, ref, send_sem, recv, target, MESH)
@@ -328,12 +335,11 @@
     def arrived(ref, recv):
         remote(ref, x_sem.at[0], recv, partner).wait_recv()
 
-    def to_partner(kind, way, unit, span):
-        recv = panel_sem.at[unit // 2] if kind == 0 else partner_sem.at[kind]
-        remote(part(kind, way, unit, span), partner_send.at[kind], recv, partner).start()
+    def to_partner(kind, ref):
+        remote(ref, partner_send.at[kind], partner_sem.at[kind], partner).start()
 
     def own(kind, i):
-        ref = part(kind, me, *z_message(kind, i))
+        ref = part(kind, me, first[i])
         recv = recv_sem.at[kind, chip, i]
 
         @pl.when(chip < chips - 1)
@@ -349,11 +355,16 @@
             far = 2 * (chips - 1 - chip) + core
             remote(ref, own_sem.at[kind, 2], recv, (far, place)).start()
 
+    def plane_send(kind, origin, k):
+        way = 2 * origin + core
+        for base, out, sem, target in ((2, x_out, x_sem, x_target), (5, y_out, y_sem, y_target)):
+            k, pair, half = out[k]
+            recv = recv_sem.at[kind, origin, base + k]
+            remote(part(kind, way, pair, half), sem.at[kind], recv, target).start()
+
     def z_step(kind, i, j):
         origin = sources[j]
-        way = 2 * origin + core
-        unit, span = z_message(kind, i)
-        ref = part(kind, way, unit, span)
+        ref = part(kind, 2 * origin + core, first[i])
         recv = recv_sem.at[kind, origin, i]
         arrived(ref, recv)
         if relays[j] is not None:
@@ -362,58 +373,63 @@
             def _():
                 remote(ref, relay_sem.at[kind, j // 2], recv, (2 * relays[j] + core, place)).start()
 
-        for k, width in plane_messages(kind, i):
-            for base, units, sem, target in ((4, x_out, x_sem, x_target), (8, y_out, y_sem, y_target)):
-                recv = recv_sem.at[kind, origin, base + k]
-                remote(part(kind, way, units[k], width), sem.at[kind], recv, target).start()
-        to_partner(kind, way, unit, span)
+        plane_send(kind, origin, 2 * i)
+        to_partner(kind, ref)
 
     def plane_step(kind, i, j):
         origin = sources[j]
         way = 2 * origin + core
-        for k, width in plane_messages(kind, i):
-            for base, units in ((4, x_in), (8, y_in)):
-                arrived(part(kind, way, units[k], width), recv_sem.at[kind, origin, base + k])
-                to_partner(kind, way, units[k], width)
-
-    stream = ((0, 0), (0, 1), (0, 2), (0, 3), (1, 0), (1, 1), (2, 0), (2, 1))
+        for ks in ((0,), (1, 2))[i : i + 1]:
+            for k in ks:
+                for base, into in ((2, x_in), (5, y_in)):
+                    _, pair, half = into[k]
+                    ref = part(kind, way, pair, half)
+                    arrived(ref, recv_sem.at[kind, origin, base + k])
+                    to_partner(kind, ref)
+        if i == 0:
+            plane_send(kind, origin, 1)
+
+    stream = [(kind, i) for kind in range(kinds) for i in range(2)]
     events = []
     for turn in range(len(stream) + 1):
         for j in range(3):
             at = turn - (j == 1)
             if 0 <= at < len(stream) and not (turn == len(stream) and j != 1):
                 events.append((at, j))
-    lag = 2
-
     def event(n):
-        def plane():
-            if lag <= n < len(events) + lag:
-                at, j = events[n - lag]
-                plane_step(*stream[at], j)
-
-        last = n == len(events) - 1
-        if last:
-            plane()
-        if n < len(events):
+        if n < 100:
             at, j = events[n]
             z_step(*stream[at], j)
-            if j == 2 and at + 2 < len(stream):
+            if at == 1 and j == 0:
+                own(*stream[2])
+            if at > 0 and j == 2 and at + 2 < len(stream):
                 own(*stream[at + 2])
-        if not last:
-            plane()
-
-    def event_of(number, first, last):
-        for n in range(first, last):
-
-            @pl.when(number == n - first)
+        else:
+            at, j = events[n - 100]
+            plane_step(*stream[at], j)
+
+    def run(*some):
+        for n in some:
+            event(n)
+
+    def plane(*some):
+        return [100 + n for n in some]
+
+    def event_of(number, lists):
+        for index, some in enumerate(lists):
+
+            @pl.when(number == index)
             def _():
-                event(n)
+                run(*some)
 
     def local_copies(kind):
-        if kind == 0:
-            for unit in range(UNITS):
-                yield conv_ref.at[:, :, pl.ds(unit * unit_cols, unit_cols)], conv_full.at[me, unit]
-        elif kind == 1:
+        if kind < GROUPS:
+            for pair in range(UNITS // 2):
+                for half in range(2):
+                    rows = pl.ds(pair * depth, depth)
+                    columns = pl.ds((2 * kind + half) * width, width)
+                    yield conv_ref.at[:, rows, columns], part(kind, me, pair, half)
+        elif kind == GROUPS:
             yield query_ref, proj_full.at[me, :, pl.ds(0, split)]
             yield keyw_ref, proj_full.at[me, :, pl.ds(split, HEAD_K)]
             yield valuew_ref, proj_full.at[me, :, pl.ds(middle, HEAD_V)]
@@ -425,34 +441,26 @@
             pltpu.make_async_copy(a, b, local_sem.at[kind]).start()
 
     def local_wait(kind):
-        whole = (conv_full, proj_full, outw_full)[kind].at[me]
+        whole = full_of(kind).at[me]
         pltpu.make_async_copy(whole, whole, local_sem.at[kind]).wait()
 
     def own_partner(kind):
-        if kind == 0:
-            for panel in range(UNITS // 2):
-                to_partner(0, me, 2 * panel, 2)
-        else:
-            to_partner(kind, me, 0, UNITS)
-
-    local_start(0)
+        to_partner(kind, full_of(kind).at[me])
+
     barrier = pltpu.get_barrier_semaphore()
     pl.semaphore_signal(barrier, inc=1, device_id=partner, device_id_type=MESH)
+    for turn in (1, chips - 1):
+        neighbour = (chip + turn) % chips * 2 + core
+        pl.semaphore_signal(barrier, inc=1, device_id=(neighbour, place), device_id_type=MESH)
     for turn in range(1, members):
         pl.semaphore_signal(
             barrier, inc=1, device_id=(me, (place + turn) % members), device_id_type=MESH
         )
-
-    for turn in (1, chips - 1):
-        neighbour = (chip + turn) % chips * 2 + core
-        pl.semaphore_signal(barrier, inc=1, device_id=(neighbour, place), device_id_type=MESH)
-    local_start(1)
-    local_start(2)
+    local_start(0)
     local_wait(0)
     pl.semaphore_wait(barrier, members + 2)
 
     own(0, 0)
-    own(0, 1)
     right = (place + 1) % members
     left = (place + members - 1) % members
     halo = [
@@ -465,53 +473,70 @@
     ]
     for copy in halo:
         copy.start()
+    stem_shift(stem_weight_ref, shifted_ref)
+    own(0, 1)
     own_partner(0)
-    local_wait(1)
-    own_partner(1)
-    local_wait(2)
-    own_partner(2)
-    stem_shift(stem_weight_ref, shifted_ref)
-    for copy in halo:
-        copy.wait()
-    low = jnp.where(place > 0, low_ref[7:8], 0)
-    high = jnp.where(place < members - 1, high_ref[0:1], 0)
-    stem_tokens(tok_ref, low, high, text_ref, hot_ref)
+    for kind in range(1, kinds):
+        local_start(kind)
+    stem_inside(tok_ref, text_ref, hot_ref)
+
+    half_dim = HEAD_K // 2
+    lane = lax.broadcasted_iota(jnp.int32, (count, HEAD_K), 1)
+    step = lane % half_dim
+    freqs = jnp.exp(step.astype(jnp.float32) * (-math.log(10000.0) / half_dim))
+    position = place * count + lax.broadcasted_iota(jnp.int32, (count, HEAD_K), 0)
+    angles = position.astype(jnp.float32) * freqs
+    turn_ref[0] = jnp.cos(angles)
+    sine = jnp.sin(angles)
+    turn_ref[1] = jnp.where(lane < half_dim, -sine, sine)
+
+    def outside():
+        for copy in halo:
+            copy.wait()
+        low = jnp.where(place > 0, low_ref[7:8], 0)
+        high = jnp.where(place < members - 1, high_ref[0:1], 0)
+        stem_outside(column_of(low, GROUP), column_of(high, GROUP), text_ref, hot_ref)
+        for kind in range(1, kinds):
+            local_wait(kind)
+            own_partner(kind)
+
+    early_events = [[n, *plane(*range(max(n - 2, 0), n - 1))] for n in range(7)]
+    early_events += [[7, *plane(5), 8, *plane(6)], []]
 
     def stem_round(r, nothing):
-        def block(j, nothing):
+        def block(step, nothing):
+            j = (step + 1) % (POOL_B + 1)
             stem_block(j, stem_bias_ref, gain_ref, ext_ref, hot_ref, shifted_ref, rows_ref)
             return nothing
 
-        lax.fori_loop(3 * r - (r + 5) // 6, 3 * r + 2, block, 0)
-        event_of(r, 0, 6)
+        lax.fori_loop(2 * r, 2 * r + 2 - r // 8, block, 0)
+        pl.when(r == 0)(outside)
+        event_of(r, early_events)
         return nothing
 
-    lax.fori_loop(0, (POOL_B + 2) // 3, stem_round, 0)
+    lax.fori_loop(0, POOL_B // 2 + 1, stem_round, 0)
     stem_edges(place, members - 1, ext_ref, rows_ref)
-    event(6)
-
-    width = 2 * unit_cols
+
     group = 8
     channels = ext_ref.shape[1]
     big = jnp.full((count, width), jnp.finfo(jnp.float32).max, jnp.float32)
 
-    def conv_panel(panel, after):
-        block_of = pl.ds(0, chips)
-        whole = conv_full.at[block_of, pl.ds(0, 2)]
-        arrived(whole, panel_sem.at[panel])
+    def conv_panel(turn, half, after):
+        weight_ref = conv_full.at[turn, :, :, half]
 
         def block(m, carry):
             most, least = carry
-            total = None
-            for tap in range(KW):
-                start = pl.multiple_of((m * group + tap) * count, count)
-                weight = jnp.concatenate(
-                    [conv_full[:, 2 * panel + h, tap].reshape(channels, unit_cols) for h in range(2)], axis=1
-                )
-                piece = jnp.dot(
-                    ext_ref[pl.ds(start, group * count), :], weight, preferred_element_type=jnp.float32
-                )
-                total = piece if total is None else total + piece
+            weight = jnp.concatenate(
+                [weight_ref[:, :, tap].reshape(channels, width) for tap in range(KW)], axis=0
+            )
+            rows = jnp.concatenate(
+                [
+                    ext_ref[pl.ds(pl.multiple_of((m * group + tap) * count, count), group * count), :]
+                    for tap in range(KW)
+                ],
+                axis=1,
+            )
+            total = jnp.dot(rows, weight, preferred_element_type=jnp.float32)
             for index in range(group):
                 piece = total[index * count : (index + 1) * count]
                 most = jnp.maximum(most, piece)
@@ -520,34 +545,49 @@
             return most, least
 
         most, least = lax.fori_loop(0, POOL_B // group, block, (-big, big))
-        at = pl.multiple_of(panel * width, width)
-        bias = conv_bias_ref[:, pl.ds(at, width)]
+        at = pl.multiple_of((2 * turn + half) * width, width)
+        bias = conv_bias_ref[pl.ds(at, width)].reshape(1, width)
         coarse_ref[:, pl.ds(at, width)] = jnp.maximum(
             jax.nn.gelu(most + bias), jax.nn.gelu(least + bias)
         ).astype(jnp.bfloat16)
 
+    late_events = [
+        [10, 11, *plane(8)],
+        [12, 13, *plane(9)],
+        [14, *plane(10, 11)],
+        [15, *plane(12)],
+        [17, 18, *plane(14)],
+        [19, *plane(15, 16)],
+        [20, 21, *plane(17)],
+        [22, *plane(18)],
+        [24, *plane(20, 21)],
+        [25, 26, *plane(22)],
+        [27, *plane(23, 24)],
+        [28, *plane(25, 26)],
+    ]
+    between = [[9, *plane(7)], [16, *plane(13)], [23, *plane(19)]]
+
     def conv_turn(t, nothing):
-        plane = (place % 2 + t % 2) % 2 + 2 * ((place // 2 + t // 2) % 2)
-        shared = t // 4
-        panel = (1 - shared) * plane + shared * (4 + (mine + t) % 2)
-        conv_panel(panel, lambda m: event_of(2 * t + m, 7, 19))
+        for turn in range(GROUPS):
+
+            @pl.when(t == 2 * turn)
+            def _():
+                run(*between[turn])
+                arrived(conv_full.at[turn, pl.ds(0, chips)], partner_sem.at[turn])
+
+        conv_panel(t // 2, t % 2, lambda m: event_of(POOL_B // group * t + m, late_events))
         return nothing
 
-    lax.fori_loop(0, UNITS // 2, conv_turn, 0)
-    event(19)
-    event(20)
-    arrived(proj_full.at[pl.ds(0, chips)], partner_sem.at[1])
+    lax.fori_loop(0, 2 * GROUPS, conv_turn, 0)
+    arrived(proj_full.at[pl.ds(0, chips)], partner_sem.at[GROUPS])
 
     def weight(begin, end):
         return proj_full[:, :, begin:end].reshape(wide, end - begin)
 
-    cosine = jnp.concatenate([cosine_ref[...], cosine_ref[...]], axis=1)
-    sine = jnp.concatenate([-sine_ref[...], sine_ref[...]], axis=1)
-
     def turned(head):
-        return (head * cosine + pltpu.roll(head, HEAD_K // 2, 1) * sine).astype(jnp.bfloat16)
-
-    hidden = rms_scale(coarse_ref[...].astype(jnp.float32), attn_gain_ref[...]).astype(
+        return (head * turn_ref[0] + pltpu.roll(head, HEAD_K // 2, 1) * turn_ref[1]).astype(jnp.bfloat16)
+
+    hidden = rms_scale(coarse_ref[...].astype(jnp.float32), attn_gain_ref[...].reshape(1, -1)).astype(
         jnp.bfloat16
     )
     key_ref[place] = turned(
@@ -570,7 +610,7 @@
             copy.start()
             pairs.append(copy)
     query = jnp.dot(hidden, weight(0, split), preferred_element_type=jnp.float32)
-    event(21)
+    run(29, *plane(27))
     for turn in range(1, members):
         spot = (place + turn) % members
         for index, ref in enumerate((key_ref, value_ref)):
@@ -590,24 +630,23 @@
         mixes.append(
             jnp.dot(weights, values, preferred_element_type=jnp.float32).astype(jnp.bfloat16)
         )
-        if head in (3, 7):
-            event(22 + head // 4)
-    for n in range(24, len(events) + lag):
-        event(n)
-    arrived(outw_full.at[pl.ds(0, chips)], partner_sem.at[2])
+        if head == 3:
+            run(*plane(28))
+    run(*plane(29))
+    arrived(outw_full.at[pl.ds(0, chips)], partner_sem.at[GROUPS + 1])
     total = coarse_ref[...].astype(jnp.float32)
     for head in range(HEADS):
         total = total + jnp.dot(mixes[head], outw_full[head], preferred_element_type=jnp.float32)
     out_ref[...] = total.astype(jnp.bfloat16)
     for copy in pairs:
         copy.wait_send()
-    for kind, full in enumerate((conv_full, proj_full, outw_full)):
-        whole = full.at[0]
+    for kind in range(kinds):
+        whole = full_of(kind).at[0]
         remote(whole, x_sem.at[kind], recv_sem.at[0, 0, 0], x_target).wait_send()
         remote(whole, y_sem.at[kind], recv_sem.at[0, 0, 0], y_target).wait_send()
-        every = full.at[pl.ds(0, chips)]
+        every = full_of(kind).at[pl.ds(0, chips)]
         remote(every, partner_send.at[kind], recv_sem.at[0, 0, 0], partner).wait_send()
-        ref = part(kind, 0, 0, 4)
+        ref = full_of(kind).at[0, pl.ds(0, 2 if kind < GROUPS else 4 * unit_rows)]
 
         @pl.when(chip < chips - 1)
         def _():
@@ -633,8 +672,8 @@
     return (
         ways == 8
         and members == 4
-        and columns == UNITS * 128
-        and depth % 16 == 0
+        and columns == 2 * GROUPS * 256
+        and depth == UNITS // 2 * 16
         and rows == HEAD_V
         and HEADS == ways
         and rows % (16 * UNITS) == 0
@@ -642,7 +681,7 @@
 
 
 def encoder_stage(
-    tokens, stem_weight, vectors, cosine, sine, conv_weight, w_query, w_key, w_value, w_out
+    tokens, stem_weight, vectors, conv_weight, w_query, w_key, w_value, w_out
 ):
     count = tokens.shape[0]
     channels = stem_weight.shape[1]
@@ -654,10 +693,11 @@
     vmem = pl.BlockSpec(memory_space=pltpu.VMEM)
     hbm = pl.BlockSpec(memory_space=pl.ANY)
     dma = pltpu.SemaphoreType.DMA
+    kinds = GROUPS + 2
     return pl.pallas_call(
         encoder_kernel,
         out_shape=jax.ShapeDtypeStruct((count, columns), jnp.bfloat16),
-        in_specs=[vmem] * 8 + [hbm] * 5,
+        in_specs=[vmem] * 6 + [hbm] * 5,
         out_specs=vmem,
         scratch_shapes=[
             pltpu.VMEM((count, columns), jnp.bfloat16),
@@ -667,31 +707,33 @@
             pltpu.VMEM((POOL_B + 1, count, GROUP), jnp.bfloat16),
             pltpu.VMEM((POOL_A, GROUP, channels), jnp.bfloat16),
             pltpu.VMEM((count, channels), jnp.float32),
+            pltpu.VMEM((2, count, HEAD_K), jnp.float32),
             pltpu.VMEM(((POOL_B + 4) * count, channels), jnp.bfloat16),
             pltpu.VMEM((8, GROUP), jnp.int32),
             pltpu.VMEM((8, GROUP), jnp.int32),
-            pltpu.VMEM((ways, UNITS, taps, depth, columns // UNITS), jnp.bfloat16),
+            pltpu.VMEM(
+                (GROUPS, ways, UNITS // 2, 2, taps, depth // 6, columns // (2 * GROUPS)), jnp.bfloat16
+            ),
             pltpu.VMEM((ways, rows, HEADS * HEAD_K + HEAD_K + HEAD_V), jnp.bfloat16),
             pltpu.VMEM((ways, rows, columns), jnp.bfloat16),
             dma((2, members)),
             dma((2, members)),
             dma((2,)),
             dma((2,)),
-            dma((3,)),
-            dma((3, chips, UNITS)),
-            dma((UNITS // 2,)),
-            dma((3,)),
-            dma((3,)),
-            dma((3,)),
-            dma((3,)),
-            dma((3, 3)),
-            dma((3, 2)),
+            dma((kinds,)),
+            dma((kinds, chips, 8)),
+            dma((kinds,)),
+            dma((kinds,)),
+            dma((kinds,)),
+            dma((kinds,)),
+            dma((kinds, 3)),
+            dma((kinds, 2)),
         ],
         compiler_params=pltpu.CompilerParams(
             collective_id=0, has_side_effects=True, vmem_limit_bytes=56 * 2**20
         ),
         name="encoder_stage",
-    )(tokens, stem_weight, *vectors, cosine, sine, conv_weight, w_query, w_key, w_value, w_out)
+    )(tokens, stem_weight, *vectors, conv_weight, w_query, w_key, w_value, w_out)
 
 
 def gather_conv(conv_weight):
@@ -742,16 +784,10 @@
     rows = w_out.shape[0]
     split = HEADS * HEAD_K
     if fits(lax.axis_size("dp"), size, conv_weight, w_query, w_out):
-        half_dim = HEAD_K // 2
-        freqs = 10000.0 ** (-jnp.arange(half_dim, dtype=jnp.float32) / half_dim)
-        positions = lax.axis_index("seq") * rows_att + jnp.arange(rows_att, dtype=jnp.int32)
-        angles = positions.astype(jnp.float32)[:, None] * freqs[None, :]
         return encoder_stage(
             tokens,
             stem_weight,
-            [vector[None] for vector in (stem_bias, conv_gain, conv_bias, attn_gain)],
-            jnp.cos(angles),
-            jnp.sin(angles),
+            [stem_bias, conv_gain, conv_bias, attn_gain],
             conv_weight,
             w_query,
             w_key,

time: 99.8 us -> 88 us (0.88)
  Pallas kernels: 91.6 us -> 85.9 us
  local copies, waits for them, and re-layouts: 6.91 us -> 1.77 us
    pallas_call x1, Pallas kernels: 91.6 us -> 85.9 us  [encoder_stage(): pl.pallas_call(encoder_kernel, out_shape=jax.ShapeDtypeStruct((count, col...]
    broadcast_in_dim x4 -> x0, local copies, waits for them, and re-layouts: 5.14 us -> none  [body(): vector[None]]
where the time goes in v2:
time: 88 us; the launch traced here: 87.7 us
  Pallas kernels  85.9 us (98%)
  local copies, waits for them, and re-layouts  1.77 us (2%)
    pallas_call x1, Pallas kernels, encoder_stage(): pl.pallas_call(encoder_kernel, out_shape=jax.ShapeDtypeStruct((count, col...  85.9 us
    unnamed x1, local copies, waits for them, and re-layouts  1.77 us

profile of v2, /device:TPU:9, one launch (start us, length us, event | category | flops | bytes accessed | tf_op | source)
XLA Modules:
  0.0 87.7 jit_solution(15950341900707155155)
XLA Ops:
  0.0 85.9 %encoder_stage.1 = bf16[128,1536]{1,0:T(8,128)(2,1)} custom-call(s32[128,128]{1,0:T(8,128)} %bitcast.3, bf16[60,768]{1,0:T(8,128)(2,1)} %stem_weight_ref.1, f32[768]{0:T(1024)} %stem_bias_ref.1, f32[768]{0:T(1024)} %gain_ref.1, f32[1536]{0:T(1024)} %conv_bias_ref.1, f32[1536]{0:T(1024)} %attn_gain_ref.1, bf16[5,96,1536]{2,1,0:T(8,128)(2,1)} %conv_ref.1, ...), custom_call_target="tpu_custom_call" | custom-call | tf_op jit(solution)/shard_map/encoder_stage/pallas_call | solution.py:697
  85.9 1.8 %copy.13 = bf16[1,128,1536]{2,1,0:T(8,128)(2,1)} copy(bf16[1,128,1536]{2,1,0:T(8,128)(2,1)} %bitcast.2) | data formatting | bytes 786432

commit v3 on v2

--- a/solution.py
+++ b/solution.py
@@ -392,7 +392,7 @@
     stream = [(kind, i) for kind in range(kinds) for i in range(2)]
     events = []
     for turn in range(len(stream) + 1):
-        for j in range(3):
+        for j in (0, 2, 1):
             at = turn - (j == 1)
             if 0 <= at < len(stream) and not (turn == len(stream) and j != 1):
                 events.append((at, j))
@@ -460,7 +460,6 @@
     local_wait(0)
     pl.semaphore_wait(barrier, members + 2)
 
-    own(0, 0)
     right = (place + 1) % members
     left = (place + members - 1) % members
     halo = [
@@ -473,6 +472,7 @@
     ]
     for copy in halo:
         copy.start()
+    own(0, 0)
     stem_shift(stem_weight_ref, shifted_ref)
     own(0, 1)
     own_partner(0)
@@ -496,8 +496,14 @@
         low = jnp.where(place > 0, low_ref[7:8], 0)
         high = jnp.where(place < members - 1, high_ref[0:1], 0)
         stem_outside(column_of(low, GROUP), column_of(high, GROUP), text_ref, hot_ref)
+
+    def loaded():
         for kind in range(1, kinds):
             local_wait(kind)
+        own_partner(1)
+
+    def passed():
+        for kind in range(2, kinds):
             own_partner(kind)
 
     early_events = [[n, *plane(*range(max(n - 2, 0), n - 1))] for n in range(7)]
@@ -510,7 +516,9 @@
             return nothing
 
         lax.fori_loop(2 * r, 2 * r + 2 - r // 8, block, 0)
-        pl.when(r == 0)(outside)
+        pl.when(r == 1)(loaded)
+        pl.when(r == 3)(outside)
+        pl.when(r == 5)(passed)
         event_of(r, early_events)
         return nothing
 
@@ -563,7 +571,7 @@
         [24, *plane(20, 21)],
         [25, 26, *plane(22)],
         [27, *plane(23, 24)],
-        [28, *plane(25, 26)],
+        [28, *plane(25)],
     ]
     between = [[9, *plane(7)], [16, *plane(13)], [23, *plane(19)]]
 
@@ -610,7 +618,7 @@
             copy.start()
             pairs.append(copy)
     query = jnp.dot(hidden, weight(0, split), preferred_element_type=jnp.float32)
-    run(29, *plane(27))
+    run(*plane(26), 29, *plane(27, 28))
     for turn in range(1, members):
         spot = (place + turn) % members
         for index, ref in enumerate((key_ref, value_ref)):
@@ -630,8 +638,6 @@
         mixes.append(
             jnp.dot(weights, values, preferred_element_type=jnp.float32).astype(jnp.bfloat16)
         )
-        if head == 3:
-            run(*plane(28))
     run(*plane(29))
     arrived(outw_full.at[pl.ds(0, chips)], partner_sem.at[GROUPS + 1])
     total = coarse_ref[...].astype(jnp.float32)
@@ -730,10 +736,10 @@
             dma((kinds, 2)),
         ],
         compiler_params=pltpu.CompilerParams(
-            collective_id=0, has_side_effects=True, vmem_limit_bytes=56 * 2**20
+            collective_id=0, has_side_effects=True, vmem_limit_bytes=40 * 2**20
         ),
         name="encoder_stage",
-    )(tokens, stem_weight, *vectors, conv_weight, w_query, w_key, w_value, w_out)
+    )(*(pltpu.with_memory_space_constraint(x, pltpu.HBM) for x in (tokens, stem_weight, *vectors, conv_weight, w_query, w_key, w_value, w_out)))
 
 
 def gather_conv(conv_weight):

time: 88 us -> 84.1 us (0.956)
  the two profiles are of different devices: /device:TPU:9 before, /device:TPU:1 now
where the time goes in v3:
time: 84.1 us; the launch traced here: 83.9 us
  Pallas kernels  83.1 us (99%)
    pallas_call x1, Pallas kernels, encoder_stage(): pl.pallas_call(encoder_kernel, out_shape=jax.ShapeDtypeStruct((count, col...  83.1 us

profile of v3, /device:TPU:1, one launch (start us, length us, event | category | flops | bytes accessed | tf_op | source)
XLA Modules:
  0.0 83.9 jit_solution(7708547767501164700)
XLA Ops:
  0.0 83.1 %encoder_stage.1 = bf16[128,1536]{1,0:T(8,128)(2,1)S(1)} custom-call(s32[128,128]{1,0:T(8,128)} %bitcast.3, bf16[60,768]{1,0:T(8,128)(2,1)} %stem_weight_ref.1, f32[768]{0:T(1024)} %stem_bias_ref.1, f32[768]{0:T(1024)} %gain_ref.1, f32[1536]{0:T(1024)} %conv_bias_ref.1, f32[1536]{0:T(1024)} %attn_gain_ref.1, bf16[5,96,1536]{2,1,0:T(8,128)(2,1)} %conv_ref.1, ...), custom_call_target="tpu_custom_call" | custom-call | tf_op jit(solution)/shard_map/encoder_stage/pallas_call | solution.py:703
  83.1 0.7 copy.13

commit v4 on v3

--- a/solution.py
+++ b/solution.py
@@ -506,8 +506,9 @@
         for kind in range(2, kinds):
             own_partner(kind)
 
-    early_events = [[n, *plane(*range(max(n - 2, 0), n - 1))] for n in range(7)]
-    early_events += [[7, *plane(5), 8, *plane(6)], []]
+    inner_events = [[n, *plane(*range(max(n - 2, 0), n - 1))] for n in range(7)]
+    inner_events += [[7, *plane(5), 8, *plane(6)], []]
+    outer_events = inner_events[:5] + [[7, *plane(3)], [*plane(4)], [5, *plane(7), 6], [8, *plane(5)]]
 
     def stem_round(r, nothing):
         def block(step, nothing):
@@ -519,7 +520,15 @@
         pl.when(r == 1)(loaded)
         pl.when(r == 3)(outside)
         pl.when(r == 5)(passed)
-        event_of(r, early_events)
+
+        @pl.when(inner)
+        def _():
+            event_of(r, inner_events)
+
+        @pl.when(jnp.logical_not(inner))
+        def _():
+            event_of(r, outer_events)
+
         return nothing
 
     lax.fori_loop(0, POOL_B // 2 + 1, stem_round, 0)
@@ -573,7 +582,9 @@
         [27, *plane(23, 24)],
         [28, *plane(25)],
     ]
-    between = [[9, *plane(7)], [16, *plane(13)], [23, *plane(19)]]
+    between = [[9], [16, *plane(13)], [23, *plane(19)]]
+    pl.when(inner)(lambda: run(*plane(7)))
+    pl.when(jnp.logical_not(inner))(lambda: run(*plane(6)))
 
     def conv_turn(t, nothing):
         for turn in range(GROUPS):

time: 84.1 us -> 83 us (0.987)
  the two profiles are of different devices: /device:TPU:1 before, /device:TPU:0 now
where the time goes in v4:
time: 83 us; the launch traced here: 82.7 us
  Pallas kernels  82 us (99%)
    pallas_call x1, Pallas kernels, encoder_stage(): pl.pallas_call(encoder_kernel, out_shape=jax.ShapeDtypeStruct((count, col...  82 us

profile of v4, /device:TPU:0, one launch (start us, length us, event | category | flops | bytes accessed | tf_op | source)
XLA Modules:
  0.0 82.7 jit_solution(2184859026843246362)
XLA Ops:
  0.0 82.0 %encoder_stage.1 = bf16[128,1536]{1,0:T(8,128)(2,1)S(1)} custom-call(s32[128,128]{1,0:T(8,128)} %bitcast.3, bf16[60,768]{1,0:T(8,128)(2,1)} %stem_weight_ref.1, f32[768]{0:T(1024)} %stem_bias_ref.1, f32[768]{0:T(1024)} %gain_ref.1, f32[1536]{0:T(1024)} %conv_bias_ref.1, f32[1536]{0:T(1024)} %attn_gain_ref.1, bf16[5,96,1536]{2,1,0:T(8,128)(2,1)} %conv_ref.1, ...), custom_call_target="tpu_custom_call" | custom-call | tf_op jit(solution)/shard_map/encoder_stage/pallas_call | solution.py:714
  82.0 0.7 copy.13

commit v5 on v4

--- a/solution.py
+++ b/solution.py
@@ -508,7 +508,8 @@
 
     inner_events = [[n, *plane(*range(max(n - 2, 0), n - 1))] for n in range(7)]
     inner_events += [[7, *plane(5), 8, *plane(6)], []]
-    outer_events = inner_events[:5] + [[7, *plane(3)], [*plane(4)], [5, *plane(7), 6], [8, *plane(5)]]
+    outer_events = inner_events[:5]
+    outer_events += [[7, *plane(3)], [*plane(4)], [5, 6], [*plane(7), 8, 9]]
 
     def stem_round(r, nothing):
         def block(step, nothing):
@@ -582,9 +583,9 @@
         [27, *plane(23, 24)],
         [28, *plane(25)],
     ]
-    between = [[9], [16, *plane(13)], [23, *plane(19)]]
-    pl.when(inner)(lambda: run(*plane(7)))
-    pl.when(jnp.logical_not(inner))(lambda: run(*plane(6)))
+    between = [[], [16, *plane(13)], [23, *plane(19)]]
+    pl.when(inner)(lambda: run(9, *plane(7)))
+    pl.when(jnp.logical_not(inner))(lambda: run(*plane(5, 6)))
 
     def conv_turn(t, nothing):
         for turn in range(GROUPS):

time: 83 us -> 82.5 us (level)
  the two profiles are of different devices: /device:TPU:0 before, /device:TPU:9 now
where the time goes in v5:
time: 82.5 us; the launch traced here: 81 us
  Pallas kernels  80.3 us (97%)
    pallas_call x1, Pallas kernels, encoder_stage(): pl.pallas_call(encoder_kernel, out_shape=jax.ShapeDtypeStruct((count, col...  80.3 us

profile of v5, /device:TPU:9, one launch (start us, length us, event | category | flops | bytes accessed | tf_op | source)
XLA Modules:
  0.0 81.0 jit_solution(10707749418663508987)
XLA Ops:
  0.0 80.3 %encoder_stage.1 = bf16[128,1536]{1,0:T(8,128)(2,1)S(1)} custom-call(s32[128,128]{1,0:T(8,128)} %bitcast.3, bf16[60,768]{1,0:T(8,128)(2,1)} %stem_weight_ref.1, f32[768]{0:T(1024)} %stem_bias_ref.1, f32[768]{0:T(1024)} %gain_ref.1, f32[1536]{0:T(1024)} %conv_bias_ref.1, f32[1536]{0:T(1024)} %attn_gain_ref.1, bf16[5,96,1536]{2,1,0:T(8,128)(2,1)} %conv_ref.1, ...), custom_call_target="tpu_custom_call" | custom-call | tf_op jit(solution)/shard_map/encoder_stage/pallas_call | solution.py:715
  80.3 0.7 copy.13
